TPU v7x, 128 devices: a whole 4x4x4 slice. The times are simulated.
128 devices in a mesh: lat: 8 (over z, core), lon: 16 (over y, x).
Axes of the slice: x: 4, y: 4, z: 4, core: 2. Of those that a mesh axis runs over, the one named last changes fastest.
Arguments:
- control: float32 [254, 64, 1536], P(None, 'lat', 'lon'), may hold values from -6 to 6
- vert_band: float32 [2, 9, 127], replicated, may hold values from -2.5 to 2.5
- lat_length: float32 [254, 8], replicated, may hold values from 3 to 32
- lon_length: float32 [254], replicated, may hold values from 3 to 192
- band_index: int32 [64], replicated, may hold values from 0 to 7
- owner_device: int32 [254, 1], replicated, may hold values from 0 to 127; in each aligned block of 254 rows (0 to 253, 254 to 507, ...) at most 4 rows name the same one
Outputs:
- winds: float32 [254, 64, 1536], P(None, 'lat', 'lon')
- slabs: float32 [512, 64, 1536], P(('lat', 'lon'))
Inputs may be any that keep to these rules, and one draw needn't show every extreme that they name: owner_device[s, 0] numbers a device along the joined axes lat+lon; no device owns more than 4 level-variables, one owns exactly 4, and every device owns at least one.
All inputs are finite; a program needn't handle non-finite values.
Results may differ from a plain program's by a relative error of at most 0.0003.
Values sent between devices are 32-bit elements; how exact they have to be, the bound alone decides.
A program may use at most 64 MiB of HBM per device.

v0:
```python
import math

import jax
import jax.numpy as jnp
from jax import lax
from jax.sharding import PartitionSpec as P

NLAT_GLOBE = 768


HIGH_ACCURACY = lax.Precision.HIGHEST


def padded(block, sides, width, periodic):
    for axis, dim in sides:
        count = lax.axis_size(axis)
        forward = [(i, i + 1) for i in range(count - 1)]
        if periodic:
            forward.append((count - 1, 0))
        backward = [(target, source) for source, target in forward]
        low = lax.ppermute(
            lax.slice_in_dim(block, block.shape[dim] - width, None, axis=dim), axis, forward
        )
        high = lax.ppermute(lax.slice_in_dim(block, 0, width, axis=dim), axis, backward)
        block = jnp.concatenate([low, block, high], axis=dim)
    return block


def slot_sources(owner_device, devices_all, most_slots):
    owners = owner_device[:, 0]
    level_ids = jnp.arange(owners.shape[0], dtype=jnp.int32)
    sharing = (owners[:, None] == owners[None, :]) & (level_ids[None, :] < level_ids[:, None])
    rank_in = jnp.sum(sharing.astype(jnp.int32), axis=1)
    slot_of = owners * most_slots + rank_in
    slot_numbers = jnp.arange(devices_all * most_slots, dtype=jnp.int32)
    matches = slot_of[None, :] == slot_numbers[:, None]
    filled = jnp.any(matches, axis=1)
    source = jnp.argmax(matches.astype(jnp.int32), axis=1)
    return (owners, rank_in, source, filled)


def rate_tables(inverse, block_len):
    slab_total, length = inverse.shape
    blocks = length // block_len
    decays = jnp.exp(-inverse)
    weights = jnp.sqrt(1.0 - decays * decays).reshape(slab_total, blocks, block_len)
    logsum = jnp.cumsum(-inverse.reshape(slab_total, blocks, block_len), axis=2)
    within = jnp.arange(block_len)
    below = within[:, None] >= within[None, :]
    spread = jnp.minimum(logsum[:, :, :, None] - logsum[:, :, None, :], 0.0)
    transfer = jnp.where(below, jnp.exp(spread), 0.0) * weights[:, :, None, :]
    return (transfer, jnp.exp(logsum))


def block_carries(gains, ends):

    def advance(running, inputs):
        gain, tail = inputs
        return (gain[:, None] * running + tail, running)

    initial = jnp.zeros_like(ends[:, 0])
    _, entries = lax.scan(advance, initial, (gains.T, jnp.moveaxis(ends, 1, 0)))
    return jnp.moveaxis(entries, 0, 1)


def sweep_rows(fields, transfer, reach):
    slab_total, length, across = fields.shape
    blocks, block_len = (reach.shape[1], reach.shape[2])
    parts = fields.reshape(slab_total, blocks, block_len, across)
    local = jnp.einsum("sbnm,sbmw->sbnw", transfer, parts, precision=HIGH_ACCURACY)
    entries = block_carries(reach[:, :, -1], local[:, :, -1, :])
    result = local + reach[:, :, :, None] * entries[:, :, None, :]
    return result.reshape(slab_total, length, across)


def sweep_cols(fields, transfer, reach):
    slab_total, across, length = fields.shape
    blocks, block_len = (reach.shape[1], reach.shape[2])
    parts = fields.reshape(slab_total, across, blocks, block_len)
    local = jnp.einsum("sbnm,swbm->swbn", transfer, parts, precision=HIGH_ACCURACY)
    entries = block_carries(reach[:, :, -1], jnp.swapaxes(local[:, :, :, -1], 1, 2))
    result = local + reach[:, None, :, :] * jnp.swapaxes(entries, 1, 2)[:, :, :, None]
    return result.reshape(slab_total, across, length)


def filter_slabs(slab, lat_inverse, lon_inverse):
    slot_total, lat_full, lon_full = slab.shape
    lat_block = math.gcd(lat_full, 128)
    lat_mats, lat_reach = rate_tables(lat_inverse, lat_block)
    northward = sweep_rows(slab, lat_mats, lat_reach)
    back_mats, back_reach = rate_tables(jnp.flip(lat_inverse, 1), lat_block)
    southward = jnp.flip(sweep_rows(jnp.flip(northward, 1), back_mats, back_reach), 1)
    lon_block = math.gcd(lon_full, 128)
    lon_table = jnp.broadcast_to(lon_inverse[:, None], (slot_total, lon_full))
    lon_mats, lon_reach = rate_tables(lon_table, lon_block)
    places = jnp.arange(lon_full, dtype=jnp.float32)
    closing = 1.0 / (1.0 - jnp.exp(-lon_full * lon_inverse))
    eastward = sweep_cols(southward, lon_mats, lon_reach)
    eastward = eastward + jnp.exp(-(places[None, :] + 1.0) * lon_inverse[:, None])[:, None, :] * (
        eastward[:, :, -1:] * closing[:, None, None]
    )
    westward = jnp.flip(sweep_cols(jnp.flip(eastward, 2), lon_mats, lon_reach), 2)
    westward = westward + jnp.exp(-(lon_full - places[None, :]) * lon_inverse[:, None])[
        :, None, :
    ] * (westward[:, :, :1] * closing[:, None, None])
    return westward


def to_owners(columns, source, filled, most_slots, lat_count, lon_count):
    level_vars, latitude_points, longitude_points = columns.shape
    devices_all = lat_count * lon_count
    by_slot = source.reshape(devices_all, most_slots).T.reshape(-1)
    live_slot = filled.reshape(devices_all, most_slots).T.reshape(-1)
    packed = jnp.where(live_slot[:, None, None], jnp.take(columns, by_slot, axis=0), 0.0)
    moved = lax.all_to_all(
        packed.reshape(most_slots, devices_all, latitude_points, longitude_points),
        ("lat", "lon"),
        split_axis=1,
        concat_axis=1,
        tiled=True,
    )
    moved = moved.reshape(most_slots, lat_count, lon_count, latitude_points, longitude_points)
    return moved.transpose(0, 1, 3, 2, 4).reshape(
        most_slots, lat_count * latitude_points, lon_count * longitude_points
    )


def into_columns(slab, owners, rank_in, lat_count, lon_count, latitude_points, longitude_points):
    most_slots = slab.shape[0]
    devices_all = lat_count * lon_count
    pieces = slab.reshape(
        most_slots, lat_count, latitude_points, lon_count, longitude_points
    ).transpose(0, 1, 3, 2, 4)
    returned = lax.all_to_all(
        pieces.reshape(most_slots, devices_all, latitude_points, longitude_points),
        ("lat", "lon"),
        split_axis=1,
        concat_axis=1,
        tiled=True,
    )
    flat_slots = returned.reshape(most_slots * devices_all, latitude_points, longitude_points)
    return jnp.take(flat_slots, rank_in * devices_all + owners, axis=0)


def winds_from(filtered, lat_pos, lat_full):
    level_vars, latitude_points, longitude_points = filtered.shape
    level_count_total = level_vars // 2
    lat_ext = padded(filtered, (("lat", 1),), 1, False)
    lon_ext = padded(filtered, (("lon", 2),), 1, True)
    d_lat = (lat_ext[:, 2:, :] - lat_ext[:, :-2, :]) * 0.5
    d_lon = (lon_ext[:, :, 2:] - lon_ext[:, :, :-2]) * 0.5
    latitude_rows = (lat_pos * latitude_points + jnp.arange(latitude_points)).astype(
        jnp.float32
    ) + float(NLAT_GLOBE - lat_full)
    latitude = jnp.pi * ((latitude_rows + 0.5) / NLAT_GLOBE - 0.5)
    metric = (1.0 / jnp.maximum(jnp.cos(latitude), 0.2))[None, :, None]
    east_wind = -d_lat[:level_count_total] + d_lon[level_count_total:] * metric
    north_wind = d_lon[:level_count_total] * metric + d_lat[level_count_total:]
    return jnp.concatenate([east_wind, north_wind], axis=0)


def shards(control, vert_band, lat_length, lon_length, band_index, owner_device):
    level_vars, latitude_points, longitude_points = control.shape
    lat_count = lax.axis_size("lat")
    lon_count = lax.axis_size("lon")
    devices_all = lat_count * lon_count
    most_slots = 2 * ((level_vars + devices_all - 1) // devices_all)
    lat_full = latitude_points * lat_count
    lat_pos = lax.axis_index("lat")
    lon_pos = lax.axis_index("lon")
    my_device = lat_pos * lon_count + lon_pos
    level_count_total = level_vars // 2
    band_width = vert_band.shape[1]
    half_band = band_width // 2
    diagonals = jnp.stack(
        [
            jnp.eye(level_count_total, k=offset - half_band, dtype=jnp.float32)
            for offset in range(band_width)
        ]
    )
    band_matrices = jnp.eye(level_count_total, dtype=jnp.float32)[None] + jnp.einsum(
        "vok,okl->vkl", vert_band, diagonals, precision=HIGH_ACCURACY
    )
    mixed = jnp.einsum(
        "jme,jet->jmt",
        band_matrices,
        control.reshape(2, level_count_total, latitude_points * longitude_points),
        precision=HIGH_ACCURACY,
    )
    mixed = mixed.reshape(level_vars, latitude_points, longitude_points)
    band_onehot = (
        band_index[None, :] == jnp.arange(lat_length.shape[1], dtype=jnp.int32)[:, None]
    ).astype(jnp.float32)
    lat_inverse = 1.0 / jnp.dot(lat_length, band_onehot, precision=HIGH_ACCURACY)
    lon_inverse = 1.0 / lon_length
    owners, rank_in, source, filled = slot_sources(owner_device, devices_all, most_slots)
    slab = to_owners(mixed, source, filled, most_slots, lat_count, lon_count)
    my_sources = lax.dynamic_slice_in_dim(source, my_device * most_slots, most_slots)
    slab_lat = jnp.take(lat_inverse, my_sources, axis=0)
    slab_lon = jnp.take(lon_inverse, my_sources, axis=0)
    slabs = filter_slabs(slab, slab_lat, slab_lon)
    filtered = into_columns(
        slabs, owners, rank_in, lat_count, lon_count, latitude_points, longitude_points
    )
    winds = winds_from(filtered, lat_pos, lat_full)
    return (winds, slabs)


def solution(mesh):
    placed = (P(None, "lat", "lon"), P(), P(), P(), P(), P())
    return jax.shard_map(
        shards,
        mesh=mesh,
        in_specs=placed,
        out_specs=(P(None, "lat", "lon"), P(("lat", "lon"), None, None)),
        check_vma=False,
    )
```

profile of v0, /device:TPU:1, one launch (start us, length us, event | category | flops | bytes accessed | tf_op | source)
XLA Modules:
  0.0 158.4 jit_solution(12169647411586467668)
XLA Ops:
  0.7 0.9 convert_reduce_fusion
  5.0 1.7 %reshape.571 = f32[2,127,768]{1,0,2:T(2,128)S(1)} reshape(f32[254,8,96]{0,2,1:T(8,128)} %param.10) | data formatting | bytes 1560576 | tf_op jit(solution)/shard_map/reshape | solution.py:187
  7.7 2.8 %stack.5 = pred[9,127,127]{2,0,1:T(8,128)(4,1)S(1)} concatenate(pred[1,127,127]{2,0,1:T(4,128)(4,1)S(1)} %iota_compare_fusion.12, pred[1,127,127]{2,0,1:T(4,128)(4,1)S(1)} %get-tuple-element.235, pred[1,127,127]{2,0,1:T(4,128)(4,1)S(1)} %get-tuple-element.234, pred[1,127,127]{2,0,1:T(4,128)(4,1)S(1)} %get-tuple-element.233, pred[1,127,127]{2,0,1:T(4,128)(4,1)S(1)} %get-tuple-element.232, ...), dimensions={0} | concatenate | bytes 290322 | tf_op jit(solution)/shard_map/stack | solution.py:175
  12.5 1.9 %gather_fusion.1 = f32[512,8,96]{2,1,0:T(8,128)S(1)} fusion(f32[254,8,96]{2,1,0:T(8,128)S(1)} %reshape.618, s32[1024]{0:T(1024)S(1)} %pad_clamp_fusion.1), kind=kCustom, calls=%fused_computation.1 | custom fusion | bytes 3147776 | tf_op jit(solution)/shard_map/jit(_take)/gather | solution.py:114
  14.4 2.7 %fusion.4 = f32[4,128,8,96]{3,2,0,1:T(8,128)} fusion(f32[4,128,8,96]{3,2,1,0:T(8,128)S(1)} %bitcast.98, pred[4,128]{0,1:T(8,128)(4,1)S(1)} %compare_and_fusion, pred[4,128]{0,1:T(8,128)(4,1)S(1)} %bitcast.104), kind=kLoop, calls=%fused_computation.18 | loop fusion | flops 786432 | bytes 3146752 | tf_op jit(solution)/shard_map/jit(_where)/select_n | solution.py:114
  17.0 11.5 %all-to-all-start = ((f32[4,128,8,96]{3,2,0,1:T(8,128)}), f32[4,128,8,96]{3,2,0,1:T(8,128)S(1)}, u32[]{:S(2)}, u32[]{:S(2)}) async-start(f32[4,128,8,96]{3,2,0,1:T(8,128)} %fusion.4), calls=%async_computation | async-start | bytes 4194304 | tf_op jit(solution)/shard_map/all_to_all | solution.py:115
  30.5 1.1 reduce_window_sum.30
  32.6 25.6 %all-to-all-done = f32[4,128,8,96]{3,2,0,1:T(8,128)S(1)} async-done(((f32[4,128,8,96]{3,2,0,1:T(8,128)}), f32[4,128,8,96]{3,2,0,1:T(8,128)S(1)}, u32[]{:S(2)}, u32[]{:S(2)}) %all-to-all-start) | async-done | bytes 1572896 | tf_op jit(solution)/shard_map/all_to_all | solution.py:115
  58.2 1.3 copy-done.1
  59.6 2.8 %copy.100 = f32[4,8,8,16,96]{4,3,2,1,0:T(8,128)S(1)} copy(f32[4,8,8,16,96]{4,2,0,3,1:T(8,128)} %bitcast.97) | data formatting | bytes 3145728 | tf_op jit(solution)/shard_map/transpose | solution.py:123
  62.4 2.1 %reshape.575 = f32[4,64,1536]{2,1,0:T(8,128)} reshape(f32[4,8,8,16,96]{4,3,2,1,0:T(8,128)S(1)} %copy.100) | data formatting | bytes 3145728 | tf_op jit(solution)/shard_map/reshape.12
  64.5 2.9 %convolution_add_fusion.1 = f32[4,64,1536]{2,1,0:T(8,128)S(1)} fusion(f32[4,64,1536]{2,1,0:T(8,128)} %reshape.575, f32[4,64]{1,0:T(4,128)S(1)} %exponential_multiply_fusion.1, f32[4,64]{1,0:T(4,128)S(1)} %get-tuple-element.208, f32[4,64]{1,0:T(4,128)S(1)} %reduce_window_sum.29, pred[64,64]{1,0:T(8,128)(4,1)S(1)} %iota_compare_fusion.13), kind=kOutput, calls=%fused_computation.16 | convolution fusion | flops 302448640 | bytes 3152896 | tf_op jit(solution)/shard_map/sbnm,sbmw->sbnw/dot_general | solution.py:70
  67.9 1.5 convolution_add_fusion
  69.5 4.2 %reverse.8 = f32[4,64,1536]{2,1,0:T(8,128)} reverse(f32[4,64,1536]{2,1,0:T(8,128)S(1)} %convolution_add_fusion), dimensions={1} | reverse | bytes 3145728 | tf_op jit(solution)/shard_map/reverse.2
  73.6 7.6 %fusion.19 = f32[4,64,12,128]{3,1,2,0:T(8,128)S(1)} fusion(f32[4]{0:T(128)S(1)} %get-tuple-element.227, f32[4,12,128]{2,1,0:T(8,128)S(1)} %reduce_window_sum.30, pred[128,128]{1,0:T(8,128)(4,1)S(1)} %iota_compare_fusion.2, f32[4,64,1536]{2,1,0:T(8,128)} %reverse.8), kind=kOutput, calls=%fused_computation.39 | convolution fusion | flops 607125504 | bytes 3186704 | tf_op jit(solution)/shard_map/sbnm,swbm->swbn/dot_general | solution.py:80
  82.2 1.4 while.6
  84.8 1.4 rev.15
  86.3 6.2 %fusion.22 = f32[4,64,12,128]{3,1,2,0:T(8,128)S(1)} fusion(f32[4]{0:T(128)S(1)} %get-tuple-element.227, f32[4,12,128]{2,1,0:T(8,128)S(1)} %reduce_window_sum.30, pred[128,128]{1,0:T(8,128)(4,1)S(1)} %iota_compare_fusion.2, f32[4,64,1536]{2,1,0:T(8,128)S(1)} %rev.15), kind=kOutput, calls=%fused_computation.40 | convolution fusion | flops 607125504 | bytes 3186704 | tf_op jit(solution)/shard_map/sbnm,swbm->swbn/dot_general | solution.py:80
  93.5 1.2 while.7
  95.4 1.4 rev.16
  96.8 1.4 multiply_add_fusion
  98.2 1.9 %reshape.581 = f32[4,8,8,16,96]{4,3,2,1,0:T(8,128)S(1)} reshape(f32[4,64,1536]{2,1,0:T(8,128)} %multiply_add_fusion) | data formatting | bytes 3145728 | tf_op jit(solution)/shard_map/reshape | solution.py:131
  101.0 1.6 %copy.112 = f32[4,128,8,96]{3,2,0,1:T(8,128)} copy(f32[4,128,8,96]{3,2,1,0:T(8,128)S(1)} %bitcast.99) | data formatting | bytes 3145728 | tf_op jit(solution)/shard_map/reshape | solution.py:135
  102.6 4.8 %all-to-all-start.1 = ((f32[4,128,8,96]{3,2,0,1:T(8,128)}), f32[4,128,8,96]{3,2,0,1:T(8,128)S(1)}, u32[]{:S(2)}, u32[]{:S(2)}) async-start(f32[4,128,8,96]{3,2,0,1:T(8,128)} %copy.112), calls=%async_computation.1 | async-start | bytes 4194304 | tf_op jit(solution)/shard_map/all_to_all | solution.py:134
  107.5 29.7 %all-to-all-done.1 = f32[4,128,8,96]{3,2,0,1:T(8,128)S(1)} async-done(((f32[4,128,8,96]{3,2,0,1:T(8,128)}), f32[4,128,8,96]{3,2,0,1:T(8,128)S(1)}, u32[]{:S(2)}, u32[]{:S(2)}) %all-to-all-start.1) | async-done | bytes 1572896 | tf_op jit(solution)/shard_map/all_to_all | solution.py:134
  137.2 1.5 copy.113
  138.7 2.3 %gather_fusion.3 = f32[254,8,96]{2,1,0:T(8,128)S(1)} fusion(f32[512,8,96]{2,1,0:T(8,128)} %bitcast.100, s32[1024]{0:T(1024)S(1)} %pad_clamp_fusion), kind=kCustom, calls=%fused_computation.3 | custom fusion | bytes 1561592 | tf_op jit(solution)/shard_map/jit(_take)/gather | solution.py:142
  142.5 3.1 %collective-permute-start = (f32[254,1,96]{2,1,0:T(1,128)}, f32[254,1,96]{2,1,0:T(1,128)S(1)}, u32[]{:S(2)}, u32[]{:S(2)}) collective-permute-start(f32[254,1,96]{2,1,0:T(1,128)} %get-tuple-element.218), channel_id=1, source_target_pairs={{16,0},{32,16},{48,32},{64,48},{80,64},{96,80},{112,96},{17,1},{33... | collective-permute-start | bytes 292616 | tf_op jit(solution)/shard_map/ppermute | solution.py:24
  145.6 2.5 %collective-permute-start.1 = (f32[254,1,96]{2,1,0:T(1,128)S(1)}, f32[254,1,96]{2,1,0:T(1,128)S(1)}, u32[]{:S(2)}, u32[]{:S(2)}) collective-permute-start(f32[254,1,96]{2,1,0:T(1,128)S(1)} %get-tuple-element.219), channel_id=1, source_target_pairs={{0,16},{16,32},{32,48},{48,64},{64,80},{80,96},{96,112},{1,17},{17... | collective-permute-start | bytes 292616 | tf_op jit(solution)/shard_map/ppermute | solution.py:21
  149.4 4.3 %collective-permute-start.2 = (f32[254,8,1]{0,1,2:T(8,128)S(1)}, f32[254,8,1]{0,1,2:T(8,128)S(1)}, u32[]{:S(2)}, u32[]{:S(2)}) collective-permute-start(f32[254,8,1]{0,1,2:T(8,128)S(1)} %copy.114), channel_id=1, source_target_pairs={{1,0},{2,1},{3,2},{4,3},{5,4},{6,5},{7,6},{8,7},{9,8},{10,9},{11,1... | collective-permute-start | bytes 24392 | tf_op jit(solution)/shard_map/ppermute | solution.py:24
  155.5 1.4 fusion.28
  157.2 1.3 copy.118
  (167 shorter events, 21.5 us)
Async XLA Ops:
  0.6 28.0 %copy-start = (f32[254,8]{0,1:T(8,128)S(1)}, f32[254,8]{0,1:T(8,128)}, u32[]{:S(2)}) copy-start(f32[254,8]{0,1:T(8,128)} %param.12) | copy-start | bytes 24388
  17.0 11.6 %copy-start.4 = (s32[64]{0:T(128)S(1)}, s32[64]{0:T(128)}, u32[]{:S(2)}) copy-start(s32[64]{0:T(128)} %param.14) | copy-start | bytes 772
  17.0 12.7 %copy-start.3 = (f32[254]{0:T(256)S(1)}, f32[254]{0:T(256)}, u32[]{:S(2)}) copy-start(f32[254]{0:T(256)} %param.13) | copy-start | bytes 3052
  17.0 41.2 %all-to-all-start = ((f32[4,128,8,96]{3,2,0,1:T(8,128)}), f32[4,128,8,96]{3,2,0,1:T(8,128)S(1)}, u32[]{:S(2)}, u32[]{:S(2)}) async-start(f32[4,128,8,96]{3,2,0,1:T(8,128)} %fusion.4), calls=%async_computation | async-start | bytes 4194304 | tf_op jit(solution)/shard_map/all_to_all | solution.py:115
  58.2 1.4 copy-start.1
  102.6 4.8 %copy-start.2 = (s32[254,1]{0,1:T(1,128)S(1)}, s32[254,1]{0,1:T(1,128)}, u32[]{:S(2)}) copy-start(s32[254,1]{0,1:T(1,128)} %param.15) | copy-start | bytes 3052
  102.6 34.6 %all-to-all-start.1 = ((f32[4,128,8,96]{3,2,0,1:T(8,128)}), f32[4,128,8,96]{3,2,0,1:T(8,128)S(1)}, u32[]{:S(2)}, u32[]{:S(2)}) async-start(f32[4,128,8,96]{3,2,0,1:T(8,128)} %copy.112), calls=%async_computation.1 | async-start | bytes 4194304 | tf_op jit(solution)/shard_map/all_to_all | solution.py:134
  142.5 12.9 %collective-permute-start = (f32[254,1,96]{2,1,0:T(1,128)}, f32[254,1,96]{2,1,0:T(1,128)S(1)}, u32[]{:S(2)}, u32[]{:S(2)}) collective-permute-start(f32[254,1,96]{2,1,0:T(1,128)} %get-tuple-element.218), channel_id=1, source_target_pairs={{16,0},{32,16},{48,32},{64,48},{80,64},{96,80},{112,96},{17,1},{33... | collective-permute-start | bytes 292616 | tf_op jit(solution)/shard_map/ppermute | solution.py:24
  145.6 9.9 %collective-permute-start.1 = (f32[254,1,96]{2,1,0:T(1,128)S(1)}, f32[254,1,96]{2,1,0:T(1,128)S(1)}, u32[]{:S(2)}, u32[]{:S(2)}) collective-permute-start(f32[254,1,96]{2,1,0:T(1,128)S(1)} %get-tuple-element.219), channel_id=1, source_target_pairs={{0,16},{16,32},{32,48},{48,64},{64,80},{80,96},{96,112},{1,17},{17... | collective-permute-start | bytes 292616 | tf_op jit(solution)/shard_map/ppermute | solution.py:21
  148.9 6.1 %collective-permute-start.3 = (f32[254,8,1]{0,1,2:T(8,128)S(1)}, f32[254,8,1]{0,1,2:T(8,128)S(1)}, u32[]{:S(2)}, u32[]{:S(2)}) collective-permute-start(f32[254,8,1]{0,1,2:T(8,128)S(1)} %copy.116), channel_id=1, source_target_pairs={{0,1},{1,2},{2,3},{3,4},{4,5},{5,6},{6,7},{7,8},{8,9},{9,10},{10,1... | collective-permute-start | bytes 24392 | tf_op jit(solution)/shard_map/ppermute | solution.py:21
  149.4 5.1 %collective-permute-start.2 = (f32[254,8,1]{0,1,2:T(8,128)S(1)}, f32[254,8,1]{0,1,2:T(8,128)S(1)}, u32[]{:S(2)}, u32[]{:S(2)}) collective-permute-start(f32[254,8,1]{0,1,2:T(8,128)S(1)} %copy.114), channel_id=1, source_target_pairs={{1,0},{2,1},{3,2},{4,3},{5,4},{6,5},{7,6},{8,7},{9,8},{10,9},{11,1... | collective-permute-start | bytes 24392 | tf_op jit(solution)/shard_map/ppermute | solution.py:24
where the time goes:
time: 159 us; the launch traced here: 158 us
  waiting for transfers between devices  56.1 us (35%)
  local copies, waits for them, and re-layouts  38.1 us (24%)
  starting transfers between devices  26.6 us (17%)
  matrix products  19.9 us (13%)
  other arithmetic  16.3 us (10%)
    all_to_all x1, waiting for transfers between devices, into_columns(): lax.all_to_all(pieces.reshape(most_slots, devices_all, latitude_points, l...  29.7 us
    all_to_all x1, waiting for transfers between devices, to_owners(): lax.all_to_all(packed.reshape(most_slots, devices_all, latitude_points, l...  25.6 us
    dot_general x2, matrix products, sweep_cols(): jnp.einsum('sbnm,swbm->swbn', transfer, parts, precision=HIGH_ACCURACY)  13.8 us
    all_to_all x1, starting transfers between devices, to_owners(): lax.all_to_all(packed.reshape(most_slots, devices_all, latitude_points, l...  11.5 us
    ppermute x2, starting transfers between devices, padded(): lax.ppermute(lax.slice_in_dim(block, 0, width, axis=dim), axis, backward)  7.38 us
    another operation x5, local copies, waits for them, and re-layouts  6.81 us
    all_to_all x1, starting transfers between devices, into_columns(): lax.all_to_all(pieces.reshape(most_slots, devices_all, latitude_points, l...  4.75 us
    dot_general x2, matrix products, sweep_rows(): jnp.einsum('sbnm,sbmw->sbnw', transfer, parts, precision=HIGH_ACCURACY)  4.42 us
  transfers between devices with their start and end apart: 6, of which 3 were waited for; matrix products, arithmetic and copies ran while one was open for 4% of the time, Pallas kernels for 0%

commit v1 on v0

v1 whole, which is shorter than its diff:
```python
import math

import jax
import jax.numpy as jnp
from jax import lax
from jax.experimental import pallas as pl
from jax.experimental.pallas import tpu as pltpu
from jax.sharding import PartitionSpec as P

NLAT_GLOBE = 768
MESH = pl.DeviceIdType.MESH
NVL = 254
NLEV = 127
LANES = 128
COLS = 96
ROWS = 8
GROUPS = 32
SLOTS = 4
CHUNKS = 2


def slot_sources(owner_device, devices_all, most_slots):
    owners = owner_device[:, 0]
    level_ids = jnp.arange(owners.shape[0], dtype=jnp.int32)
    sharing = (owners[:, None] == owners[None, :]) & (level_ids[None, :] < level_ids[:, None])
    rank_in = jnp.sum(sharing.astype(jnp.int32), axis=1)
    slot_of = owners * most_slots + rank_in
    slot_numbers = jnp.arange(devices_all * most_slots, dtype=jnp.int32)
    matches = slot_of[None, :] == slot_numbers[:, None]
    return NVL + jnp.sum(jnp.where(matches, level_ids[None, :] - NVL, 0), axis=1)


def iota(shape, dim):
    return lax.broadcasted_iota(jnp.int32, shape, dim)


def spread(column):
    return jnp.broadcast_to(column, (8, LANES))


def columns_kernel(
    source_ref,
    band_ref,
    table_ref,
    control_ref,
    arrived_ref,
    winds_ref,
    control_in,
    padded,
    mixed,
    field,
    final,
    whole,
    slopes,
    lat_inv,
    lon_send,
    lon_recv,
    lon_acc,
    to_partner,
    own_out,
    near_recv,
    chip_send,
    chip_recv,
    in_send,
    in_recv,
    north_end,
    blocks_out,
    in_sem,
    lon_sems,
    near_sems,
    chip_send_sems,
    chip_recv_sems,
    far_sems,
    all_sems,
):
    lat = lax.axis_index("lat")
    lon = lax.axis_index("lon")
    z, core = lat // 2, lat % 2
    y, x = lon // 4, lon % 4
    me = lat * 16 + lon
    partner = (z * 2 + 1 - core, lon)

    barrier = pltpu.get_barrier_semaphore()

    @pl.loop(1, 16)
    def _(i):
        pl.semaphore_signal(
            barrier, inc=1, device_id=(lat, lax.rem(lon + i, 16)), device_id_type=MESH
        )

    @pl.loop(1, 8)
    def _(i):
        pl.semaphore_signal(
            barrier, inc=1, device_id=(lax.rem(lat + i, 8), lon), device_id_type=MESH
        )

    load = pltpu.make_async_copy(control_ref, control_in, in_sem)
    load.start()

    lane = iota((8, LANES), 1)
    lane_f = lane.astype(jnp.float32)

    band_row = jnp.broadcast_to(table_ref[256:257, :], (8, LANES))

    @pl.loop(0, GROUPS)
    def _(g):
        rows = pl.ds(pl.multiple_of(g * 8, 8), 8)
        lengths = table_ref[rows, :]
        chosen = jnp.ones((8, LANES), jnp.float32)
        for b in range(8):
            chosen = jnp.where(band_row == float(b), spread(lengths[:, b : b + 1]), chosen)
        lat_inv[rows, :] = jnp.where(lane < 64, 1.0 / chosen, 0.0)

    zero_tile = jnp.zeros((8, LANES), jnp.float32)

    @pl.loop(0, 2 * 135)
    def _(r):
        padded[r] = zero_tile

    load.wait()

    for v in range(2):

        @pl.loop(0, NLEV)
        def _(k):
            padded[v * 135 + 4 + k, :, 0:COLS] = control_in[v * NLEV + k]

    for v in range(2):

        @pl.loop(0, NLEV)
        def _(k):
            total = padded[v * 135 + 4 + k]
            for o in range(9):
                total = total + band_ref[v, o, k] * padded[v * 135 + k + o]
            mixed[pl.ds(pl.multiple_of((v * NLEV + k) * 8, 8), 8), :] = pltpu.roll(total, 1, 1)

    mixed[NVL * 8 : NVL * 8 + 8, :] = zero_tile
    mixed[NVL * 8 + 8 : NVL * 8 + 16, :] = zero_tile

    lane16 = lane % 16

    def lon_rate(rows):
        return 1.0 / spread(table_ref[rows, 8:9])

    @pl.loop(0, GROUPS)
    def _(g):
        rows = pl.ds(pl.multiple_of(g * 8, 8), 8)
        inv = lon_rate(rows)
        east_factor, west_factor = [], []
        for k in range(7):
            step = 1 << k
            power = jnp.exp(-float(step) * inv)
            east_factor.append(jnp.where(lane >= step, power, 0.0))
            west_factor.append(jnp.where(lane < LANES - step, power, 0.0))
        states = jnp.zeros((8, LANES), jnp.float32)
        for j in range(8):
            values = mixed[pl.ds(g * 64 + j, 8, stride=8), :]
            east, west = values, values
            for k in range(7):
                step = 1 << k
                east = east + east_factor[k] * pltpu.roll(east, step, 1)
                west = west + west_factor[k] * pltpu.roll(west, LANES - step, 1)
            field[pl.ds(pl.multiple_of(g * 64 + j * 8, 8), 8), :] = east + west - values
            states = jnp.where(lane16 == j, spread(east[:, 96:97]), states)
            states = jnp.where(lane16 == 8 + j, spread(west[:, 1:2]), states)
        part = pl.ds(pl.multiple_of((g // 8) * 8, 8), 8)
        lon_send[part, :] = jnp.where(lane // 16 == g % 8, states, lon_send[part, :])

    pl.semaphore_wait(barrier, 22)

    @pl.loop(1, 16)
    def _(i):
        pltpu.make_async_remote_copy(
            src_ref=lon_send,
            dst_ref=lon_recv.at[lon],
            send_sem=lon_sems.at[0],
            recv_sem=lon_sems.at[1],
            device_id=(lat, lax.rem(lon + i, 16)),
            device_id_type=MESH,
        ).start()

    is_east = lane16 < 8
    for t in range(4):
        inv = jnp.zeros((8, LANES), jnp.float32)
        for b in range(8):
            g = t * 8 + b
            inv = jnp.where(lane // 16 == b, lon_rate(pl.ds(g * 8, 8)), inv)
        lon_acc[32 + t * 8 : 40 + t * 8, :] = inv

    fifteen = lon_recv.at[pl.ds(0, 15)]
    pltpu.make_async_copy(fifteen, fifteen, lon_sems.at[1]).wait()

    for t in range(4):
        part = slice(t * 8, t * 8 + 8)
        inv = lon_acc[32 + t * 8 : 40 + t * 8, :]
        total = lon_send[part, :] * jnp.exp(-(96.0 * 15.0) * inv)
        for dq in range(1, 16):
            got = lon_recv[lax.rem(lon + 16 - dq, 16), part, :]
            blocks = jnp.where(is_east, float(dq - 1), float(15 - dq))
            total = total + got * jnp.exp(-96.0 * blocks * inv)
        lon_acc[part, :] = total / (1.0 - jnp.exp(-1536.0 * inv))

    lat_lane = lane
    first_row = lat * 8
    partner_first = (z * 2 + 1 - core) * 8

    def lat_rates(rows):
        return lat_inv[rows, :]

    def total_between(rates, low, high):
        inside = (lat_lane >= low) & (lat_lane < high)
        return jnp.exp(-jnp.sum(jnp.where(inside, rates, 0.0), axis=1, keepdims=True))

    def own_factors(rates):
        own = pltpu.roll(rates, lax.rem(LANES - first_row, LANES), 1)
        decay = jnp.exp(-own)
        return decay, jnp.sqrt(1.0 - decay * decay)

    def reflection(rates):
        beyond = jnp.where(lat_lane >= first_row + 8, rates, 0.0)
        running = beyond
        for k in range(6):
            step = 1 << k
            running = running + jnp.where(lat_lane >= step, pltpu.roll(running, step, 1), 0.0)
        decay = jnp.exp(-rates)
        weight = jnp.sqrt(1.0 - decay * decay)
        terms = weight * jnp.exp(-(2.0 * running - rates))
        inside = (lat_lane >= first_row + 8) & (lat_lane < 64)
        return jnp.sum(jnp.where(inside, terms, 0.0), axis=1, keepdims=True)

    span = GROUPS // CHUNKS

    def rows_of(g):
        return pl.ds(pl.multiple_of(g * 8, 8), 8)

    def chunk_rows(c):
        return pl.ds(c * span * 8, span * 8)

    def exchange(src, dst, c, sems):
        return pltpu.make_async_remote_copy(
            src_ref=src.at[chunk_rows(c)],
            dst_ref=dst.at[chunk_rows(c)],
            send_sem=sems.at[0, c],
            recv_sem=sems.at[1, c],
            device_id=partner,
            device_id_type=MESH,
        )

    near = [exchange(to_partner, near_recv, c, near_sems) for c in range(CHUNKS)]
    far = [exchange(in_send, in_recv, c, far_sems) for c in range(CHUNKS)]
    toward = jnp.where(core == 1, 1, -1)

    def chip_copy(c, d):
        target = z + toward * d
        return pltpu.make_async_remote_copy(
            src_ref=chip_send.at[chunk_rows(c)],
            dst_ref=chip_recv.at[d - 1, chunk_rows(c)],
            send_sem=chip_send_sems.at[c, d - 1],
            recv_sem=chip_recv_sems.at[c, d - 1],
            device_id=(target * 2 + core, lon),
            device_id_type=MESH,
        )

    def target_there(d):
        target = z + toward * d
        return (target >= 0) & (target < 4)

    def sender_there(d):
        sender = z - toward * d
        return (sender >= 0) & (sender < 4)

    for c in range(CHUNKS):

        @pl.loop(c * span, (c + 1) * span)
        def _(g):
            rows = rows_of(g)
            inv = lon_rate(rows)
            east_power = jnp.exp(-inv * lane_f)
            west_power = jnp.exp(-inv * jnp.maximum(97.0 - lane_f, 0.0))
            part = pl.ds(pl.multiple_of((g // 8) * 8, 8), 8)
            arriving = pltpu.roll(lon_acc[part, :], lax.rem(LANES - (g % 8) * 16, LANES), 1)
            rates = lat_rates(rows)
            decay, weight = own_factors(rates)
            north = jnp.zeros((8, LANES), jnp.float32)
            values = []
            for j in range(8):
                at = pl.ds(pl.multiple_of(g * 64 + j * 8, 8), 8)
                value = (
                    field[at, :]
                    + spread(arriving[:, j : j + 1]) * east_power
                    + spread(arriving[:, 8 + j : 9 + j]) * west_power
                )
                field[at, :] = value
                north = spread(decay[:, j : j + 1]) * north + spread(weight[:, j : j + 1]) * value
                values.append(north)
            south = jnp.zeros((8, LANES), jnp.float32)
            for j in reversed(range(8)):
                south = (
                    spread(decay[:, j : j + 1]) * south + spread(weight[:, j : j + 1]) * values[j]
                )
            through = total_between(rates, first_row, first_row + 8)
            southbound = south + spread(through * reflection(rates)) * north
            north_end[rows, :] = north
            to_partner[rows, :] = jnp.where(core == 0, north, southbound)
            own_out[rows, :] = jnp.where(core == 0, southbound, north)

        near[c].start()

    for c in range(CHUNKS):
        near[c].wait_recv()

        @pl.loop(c * span, (c + 1) * span)
        def _(g):
            rows = rows_of(g)
            through = total_between(lat_rates(rows), first_row, first_row + 8)
            chip_send[rows, :] = own_out[rows, :] + spread(through) * near_recv[rows, :]

        for d in range(1, 4):

            @pl.when(target_there(d))
            def _():
                chip_copy(c, d).start()

    for c in range(CHUNKS):
        for d in range(1, 4):

            @pl.when(sender_there(d))
            def _():
                chip_copy(c, d).wait_recv()

        @pl.loop(c * span, (c + 1) * span)
        def _(g):
            rows = rows_of(g)
            rates = lat_rates(rows)
            total = jnp.zeros((8, LANES), jnp.float32)
            for d in range(1, 4):
                low = jnp.where(core == 1, z - d + 1, z + 1) * 16
                high = jnp.where(core == 1, z, z + d) * 16
                factor = spread(total_between(rates, low, high))
                total = total + jnp.where(
                    sender_there(d), factor * chip_recv[d - 1, rows, :], 0.0
                )
            in_send[rows, :] = total

        far[c].start()

    for c in range(CHUNKS):
        far[c].wait_recv()

        @pl.loop(c * span, (c + 1) * span)
        def _(g):
            rows = rows_of(g)
            rates = lat_rates(rows)
            decay, weight = own_factors(rates)
            past = total_between(rates, partner_first, partner_first + 8)
            nearer = near_recv[rows, :] + spread(past) * in_send[rows, :]
            farther = in_recv[rows, :]
            north_in = jnp.where(core == 1, nearer, farther)
            south_sum = jnp.where(core == 1, farther, nearer)
            through = total_between(rates, first_row, first_row + 8)
            north_out = north_end[rows, :] + spread(through) * north_in
            south_in = south_sum + spread(reflection(rates)) * north_out
            north = north_in
            values = []
            for j in range(8):
                at = pl.ds(pl.multiple_of(g * 64 + j * 8, 8), 8)
                north = (
                    spread(decay[:, j : j + 1]) * north
                    + spread(weight[:, j : j + 1]) * field[at, :]
                )
                values.append(north)
            south = south_in
            results = [None] * 8 + [south_in]
            for j in reversed(range(8)):
                south = (
                    spread(decay[:, j : j + 1]) * south + spread(weight[:, j : j + 1]) * values[j]
                )
                results[j] = south
            below = (
                spread(decay[:, LANES - 1 : LANES]) * results[0]
                + spread(weight[:, LANES - 1 : LANES]) * north_in
            )
            below = jnp.where(lat == 0, 0.0, below)
            for j in range(8):
                final[pl.ds(g * 64 + j, 8, stride=8), :] = results[j]
                lower = below if j == 0 else results[j - 1]
                slopes[pl.ds(g * 64 + j, 8, stride=8), :] = (results[j + 1] - lower) * 0.5
            for j in range(8):
                whole[g * 8 + j] = final[pl.ds(pl.multiple_of(g * 64 + j * 8, 8), 8), :]

    quarter = x
    base = lax.rem(96 * quarter + 127, LANES)
    free = lane // 32 == 3 - quarter

    def pack(dest):
        def slot(i):
            return whole[source_ref[dest * SLOTS + i]]

        last = slot(3)
        for i in range(3):
            piece = pltpu.roll(slot(i), base, 1)
            extra = pltpu.roll(last, lax.rem(base + 32 * (3 - i), LANES), 1)
            blocks_out[dest, :, i * LANES : (i + 1) * LANES] = jnp.where(free, extra, piece)

    def place(o):
        oz, oc, oy, ox = o // 32, (o // 16) % 2, (o // 4) % 4, o % 4
        tlat = lax.rem(z + oz, 4) * 2 + lax.rem(core + oc, 2)
        tlon = lax.rem(y + oy, 4) * 4 + lax.rem(x + ox, 4)
        return tlat, tlon

    @pl.loop(1, 128)
    def _(i):
        tlat, tlon = place(lax.rem(i * 45, 128))
        dest = tlat * 16 + tlon
        pack(dest)
        pltpu.make_async_remote_copy(
            src_ref=blocks_out.at[dest],
            dst_ref=arrived_ref.at[me],
            send_sem=all_sems.at[0],
            recv_sem=all_sems.at[1],
            device_id=(tlat, tlon),
            device_id_type=MESH,
        ).start()

    pack(me)
    kept = pltpu.make_async_copy(blocks_out.at[me], arrived_ref.at[me], all_sems.at[2])
    kept.start()

    row = (first_row + iota((8, LANES), 0)).astype(jnp.float32) + float(NLAT_GLOBE - 64)
    latitude = math.pi * ((row + 0.5) / NLAT_GLOBE - 0.5)
    metric = 0.5 / jnp.maximum(jnp.cos(latitude), 0.2)

    @pl.loop(0, NLEV)
    def _(k):
        one = pl.ds(pl.multiple_of(k * 8, 8), 8)
        two = pl.ds(pl.multiple_of((k + NLEV) * 8, 8), 8)
        rot, div = final[one, :], final[two, :]
        rot_lon = pltpu.roll(rot, LANES - 2, 1) - rot
        div_lon = pltpu.roll(div, LANES - 2, 1) - div
        rot_lat = pltpu.roll(slopes[one, :], LANES - 1, 1)
        div_lat = pltpu.roll(slopes[two, :], LANES - 1, 1)
        padded[k] = div_lon * metric - rot_lat
        padded[k + NLEV] = rot_lon * metric + div_lat

    kept_winds = pltpu.make_async_copy(padded.at[pl.ds(0, NVL)], winds_ref, in_sem)
    kept_winds.start()

    pltpu.make_async_copy(fifteen, fifteen, lon_sems.at[0]).wait()
    for c in range(CHUNKS):
        near[c].wait_send()
        far[c].wait_send()
        for d in range(1, 4):

            @pl.when(target_there(d))
            def _():
                chip_copy(c, d).wait_send()

    kept.wait()
    kept_winds.wait()
    others = blocks_out.at[pl.ds(0, 127)]
    landed = arrived_ref.at[pl.ds(0, 127)]
    pltpu.make_async_copy(others, others, all_sems.at[0]).wait()
    pltpu.make_async_copy(landed, landed, all_sems.at[1]).wait()


def slabs_kernel(arrived_ref, winds_in_ref, slabs_ref, winds_ref):
    lane = iota((8, LANES), 1)
    block = lane // 32
    for g in range(4):
        got = [
            [arrived_ref[4 * g + l, :, c * LANES : (c + 1) * LANES] for c in range(3)]
            for l in range(4)
        ]

        def put(slot, v, value):
            at = (g * 3 + v) * LANES
            slabs_ref[slot, :, at : at + LANES] = value

        moved = []
        for c in range(3):
            for v, width in enumerate((96, 64, 32)):
                put(c, v, jnp.where(lane < width, got[v][c], got[v + 1][c]))
            merged = jnp.where(
                block == 3,
                got[0][c],
                jnp.where(block == 2, got[1][c], jnp.where(block == 1, got[2][c], got[3][c])),
            )
            moved.append(pltpu.roll(merged, 32 * (c + 1), 1))
        for v in range(3):
            parts = [moved[(4 * v + b) % 3] for b in range(4)]
            value = jnp.where(
                block == 0,
                parts[0],
                jnp.where(block == 1, parts[1], jnp.where(block == 2, parts[2], parts[3])),
            )
            put(3, v, value)
    winds_ref[...] = winds_in_ref[:, :, 0:COLS]


def shards(control, vert_band, lat_length, lon_length, band_index, owner_device):
    source = slot_sources(owner_device, 128, SLOTS)
    lengths = jnp.concatenate([lat_length, lon_length[:, None]], axis=1)
    table = jnp.pad(lengths, ((0, 10), (0, LANES - 9)), constant_values=1.0)
    band = jnp.pad(band_index.astype(jnp.float32), (0, 64))
    table = jnp.where(jnp.arange(264)[:, None] == 256, band[None, :], table)
    vmem = pltpu.VMEM
    f32 = jnp.float32
    level = (256, LANES)
    arrived, winds_wide = pl.pallas_call(
        columns_kernel,
        out_shape=(
            jax.ShapeDtypeStruct((128, 8, 3 * LANES), f32),
            jax.ShapeDtypeStruct((NVL, 8, LANES), f32),
        ),
        in_specs=[
            pl.BlockSpec(memory_space=pltpu.SMEM),
            pl.BlockSpec(memory_space=pltpu.SMEM),
            pl.BlockSpec(memory_space=vmem),
            pl.BlockSpec(memory_space=pl.ANY),
        ],
        out_specs=(pl.BlockSpec(memory_space=pl.ANY), pl.BlockSpec(memory_space=pl.ANY)),
        scratch_shapes=[
            vmem((NVL, 8, COLS), f32),
            vmem((2 * 135, 8, LANES), f32),
            vmem((2048, LANES), f32),
            vmem((2048, LANES), f32),
            vmem((2048, LANES), f32),
            vmem((256, 8, LANES), f32),
            vmem((2048, LANES), f32),
            vmem(level, f32),
            vmem((32, LANES), f32),
            vmem((16, 32, LANES), f32),
            vmem((64, LANES), f32),
            vmem(level, f32),
            vmem(level, f32),
            vmem(level, f32),
            vmem(level, f32),
            vmem((3,) + level, f32),
            vmem(level, f32),
            vmem(level, f32),
            vmem(level, f32),
            vmem((128, 8, 3 * LANES), f32),
            pltpu.SemaphoreType.DMA,
            pltpu.SemaphoreType.DMA((2,)),
            pltpu.SemaphoreType.DMA((2, CHUNKS)),
            pltpu.SemaphoreType.DMA((CHUNKS, 3)),
            pltpu.SemaphoreType.DMA((CHUNKS, 3)),
            pltpu.SemaphoreType.DMA((2, CHUNKS)),
            pltpu.SemaphoreType.DMA((3,)),
        ],
        compiler_params=pltpu.CompilerParams(collective_id=0, has_side_effects=True),
        name="columns",
    )(source, vert_band, table, control)
    slabs, winds = pl.pallas_call(
        slabs_kernel,
        grid=(8,),
        out_shape=(
            jax.ShapeDtypeStruct((SLOTS, 64, 1536), f32),
            jax.ShapeDtypeStruct((NVL, 8, COLS), f32),
        ),
        in_specs=[
            pl.BlockSpec((16, 8, 3 * LANES), lambda i: (i, 0, 0)),
            pl.BlockSpec((32, 8, LANES), lambda i: (i, 0, 0)),
        ],
        out_specs=(
            pl.BlockSpec((SLOTS, 8, 1536), lambda i: (0, i, 0)),
            pl.BlockSpec((32, 8, COLS), lambda i: (i, 0, 0)),
        ),
        name="slabs",
    )(arrived, winds_wide)
    return (winds, slabs)


def solution(mesh):
    placed = (P(None, "lat", "lon"), P(), P(), P(), P(), P())
    return jax.shard_map(
        shards,
        mesh=mesh,
        in_specs=placed,
        out_specs=(P(None, "lat", "lon"), P(("lat", "lon"), None, None)),
        check_vma=False,
    )
```

time: 159 us -> 140 us (0.88)
  Pallas kernels: 0 us -> 128 us
  waiting for transfers between devices: 56.1 us -> 0 us
  local copies, waits for them, and re-layouts: 38.1 us -> 6.33 us
  starting transfers between devices: 26.6 us -> 0 us
  matrix products: 19.9 us -> 0 us
  other arithmetic: 16.3 us -> 4.5 us
    pallas_call x0 -> x2, Pallas kernels: none -> 128 us  [the longest x1 122 us: shards(): pl.pallas_call(columns_kernel, out_shape=(jax.ShapeDtypeStruct((128, 8, 3...]
    all_to_all x2 -> x0, waiting for transfers between devices: 55.3 us -> none  [the longest x1 29.7 us: into_columns(): lax.all_to_all(pieces.reshape(most_slots, devices_all, latitude_points, l...]
    dot_general x7 -> x0, matrix products: 19.9 us -> none  [the longest x2 13.8 us: sweep_cols(): jnp.einsum('sbnm,swbm->swbn', transfer, parts, precision=HIGH_ACCURACY)]
    all_to_all x2 -> x0, starting transfers between devices: 16.2 us -> none  [the longest x1 11.5 us: to_owners(): lax.all_to_all(packed.reshape(most_slots, devices_all, latitude_points, l...]
    ppermute x4 -> x0, starting transfers between devices: 10.4 us -> none  [the longest x2 7.38 us: padded(): lax.ppermute(lax.slice_in_dim(block, 0, width, axis=dim), axis, backward)]
    another operation x8 -> x0, local copies, waits for them, and re-layouts: 9.62 us -> none
    reshape x8 -> x0, local copies, waits for them, and re-layouts: 6.89 us -> none  [the longest x2 2.8 us: into_columns(): slab.reshape(most_slots, lat_count, latitude_points, lon_count, longitude...]
    gather x4 -> x0, local copies, waits for them, and re-layouts: 5.44 us -> none  [the longest x1 2.34 us: into_columns(): return jnp.take(flat_slots, rank_in * devices_all + owners, axis=0)]
  transfers between devices with their start and end apart: 6 -> 0, of which waited for: 3 -> 0; matrix products, arithmetic and copies ran while one was open for 4% -> 0% of each run, Pallas kernels for 0% -> 0%
where the time goes in v1:
time: 140 us; the launch traced here: 139 us
  Pallas kernels  128 us (91%)
  local copies, waits for them, and re-layouts  6.33 us (5%)
  other arithmetic  4.5 us (3%)
    pallas_call x1, Pallas kernels, shards(): pl.pallas_call(columns_kernel, out_shape=(jax.ShapeDtypeStruct((128, 8, 3...  122 us
    pallas_call x1, Pallas kernels, shards(): pl.pallas_call(slabs_kernel, grid=(8,), out_shape=(jax.ShapeDtypeStruct((...  6.25 us
    unnamed x3, local copies, waits for them, and re-layouts  6.21 us

profile of v1, /device:TPU:1, one launch (start us, length us, event | category | flops | bytes accessed | tf_op | source)
XLA Modules:
  0.0 139.4 jit_solution(1753962341650069383)
XLA Ops:
  0.6 0.7 convert_element_type.9
  1.3 0.9 convert_reduce_fusion
  2.2 0.7 iota_add_fusion
  2.9 0.2 select_reduce_fusion
  3.1 0.6 broadcast_add_fusion.source_ref
  3.7 1.3 copy.22.band_ref
  5.0 0.7 pad_maximum_fusion
  5.7 0.1 copy.21
  5.8 0.8 pad_select_fusion.table_ref
  6.6 2.5 %copy.23.control_ref = f32[254,8,96]{2,1,0:T(8,128)} copy(f32[254,8,96]{0,2,1:T(8,128)} %param.6) | data formatting | bytes 1560576 | tf_op args[0]
  9.0 121.7 %columns.1 = (f32[128,8,384]{2,1,0:T(8,128)}, f32[254,8,128]{2,1,0:T(8,128)}) custom-call(s32[512]{0:T(512)} %broadcast_add_fusion.source_ref, f32[2,9,127]{2,1,0:T(8,128)} %copy.22.band_ref, f32[264,128]{1,0:T(8,128)} %pad_select_fusion.table_ref, f32[254,8,96]{2,1,0:T(8,128)} %copy.23.control_ref), custom_call_target="tpu_custom_call" | custom-call | tf_op jit(solution)/shard_map/columns/pallas_call | solution.py:509
  130.7 6.3 %slabs.1 = (f32[4,64,1536]{2,1,0:T(8,128)}, f32[254,8,96]{2,1,0:T(8,128)}) custom-call(f32[128,8,384]{2,1,0:T(8,128)} %get-tuple-element.6.arrived_ref, f32[254,8,128]{2,1,0:T(8,128)} %get-tuple-element.7.winds_in_ref), custom_call_target="tpu_custom_call" | custom-call | tf_op jit(solution)/shard_map/slabs/pallas_call | solution.py:554
  137.0 2.4 %copy.24 = f32[254,8,96]{0,2,1:T(8,128)} copy(f32[254,8,96]{2,1,0:T(8,128)} %get-tuple-element.16) | data formatting | bytes 1560576
  (2 shorter events, 0.0 us)

commit v2 on v1

v2 whole, which is shorter than its diff:
```python
import math

import jax
import jax.numpy as jnp
from jax import lax
from jax.experimental import pallas as pl
from jax.experimental.pallas import tpu as pltpu
from jax.sharding import PartitionSpec as P

NLAT_GLOBE = 768
MESH = pl.DeviceIdType.MESH
NLEV = 127
LANES = 128
WIDE = 256
COLS = 96
SLOTS = 4
STEPS = 12
HIGH = 104
CHUNKS = ((0, 6), (6, 13))
BATCHES = 2
SPREAD = 45
BF = jnp.bfloat16
F32 = jnp.float32


def iota(shape, dim):
    return lax.broadcasted_iota(jnp.int32, shape, dim)


def wide(row):
    return jnp.broadcast_to(row, (8, WIDE))


def tile(index):
    return pl.ds(pl.multiple_of(index * 8, 8), 8)


def strided(ref, start, stride, half):
    return jnp.concatenate(
        [ref[pl.ds(start + t * half, 8, stride=stride), :] for t in range(2)], axis=1
    )


def row_of(ref, index):
    return jnp.concatenate([ref[pl.ds(index + t * 64, 1), :] for t in range(2)], axis=1)


def split(value):
    high = value.astype(BF)
    return high, (value - high.astype(F32)).astype(BF)


def columns_kernel(
    band_index_ref,
    table_ref,
    control_ref,
    arrived_ref,
    winds_ref,
    control_in,
    parts_high,
    parts_low,
    band_high,
    band_low,
    mixed,
    field,
    slopes,
    natural,
    turned_high,
    turned_low,
    picks,
    by_slot,
    blocks_out,
    lengths,
    decays,
    weights,
    own_decay,
    own_weight,
    small,
    metrics,
    powers,
    east_in,
    west_in,
    lon_send,
    lon_recv,
    lon_total,
    to_partner,
    own_out,
    near_recv,
    chip_send,
    chip_recv,
    in_send,
    in_recv,
    north_end,
    in_sem,
    lon_sems,
    near_sems,
    chip_send_sems,
    chip_recv_sems,
    far_sems,
    all_sems,
):
    lat = lax.axis_index("lat")
    lon = lax.axis_index("lon")
    z, core = lat // 2, lat % 2
    y, x = lon // 4, lon % 4
    me = lat * 16 + lon
    partner = (z * 2 + 1 - core, lon)
    first_row = lat * 8

    barrier = pltpu.get_barrier_semaphore()

    @pl.loop(1, 16)
    def _(i):
        pl.semaphore_signal(
            barrier, inc=1, device_id=(lat, lax.rem(lon + i, 16)), device_id_type=MESH
        )

    @pl.loop(1, 8)
    def _(i):
        pl.semaphore_signal(
            barrier, inc=1, device_id=(lax.rem(lat + i, 8), lon), device_id_type=MESH
        )

    load = pltpu.make_async_copy(control_ref, control_in, in_sem)
    load.start()

    row8 = iota((8, WIDE), 0)
    lane = iota((8, LANES), 1)

    column = iota((8, WIDE), 1)
    kind = column // LANES
    level = column % LANES
    place_of = kind * NLEV + level
    real = level < NLEV
    targets = []
    for o in range(9):
        inside = (level + (o - 4) >= 0) & (level + (o - 4) < NLEV) & real
        targets.append(jnp.where(inside, place_of + (o - 4), -1))
    bands = [wide(table_ref[16 + o : 17 + o, :]) for o in range(9)]
    bands[4] = bands[4] + 1.0

    @pl.loop(0, 16)
    def _(r):
        pair = []
        for h in range(2):
            row = row8 + r * 16 + h * 8
            total = jnp.zeros((8, WIDE), F32)
            for o in range(9):
                total = jnp.where(targets[o] == row, bands[o], total)
            pair.append(total)
        high, low = split(jnp.concatenate(pair, axis=0))
        at = pl.ds(pl.multiple_of(r * 16, 16), 16)
        band_high[at, :] = high
        band_low[at, :] = low

    load.wait()

    @pl.loop(0, 8)
    def _(j):
        value = control_in[j]
        high, low = split(value)
        at = pl.ds(pl.multiple_of(j * COLS, 16), COLS)
        parts_high[at, :] = jnp.zeros((COLS, WIDE), BF)
        parts_low[at, :] = jnp.zeros((COLS, WIDE), BF)
        parts_high[at, 0:254] = high
        parts_low[at, 0:254] = low

    for h in range(2):
        at = slice(h * 384, h * 384 + 384)
        product = (
            jnp.dot(parts_high[at, :], band_high[...], preferred_element_type=F32)
            + jnp.dot(parts_high[at, :], band_low[...], preferred_element_type=F32)
            + jnp.dot(parts_low[at, :], band_high[...], preferred_element_type=F32)
        )
        for t in range(2):
            put = slice(t * 768 + h * 384, t * 768 + h * 384 + 384)
            mixed[put, :] = product[:, t * LANES : t * LANES + LANES]

    inv = 1.0 / wide(table_ref[8:9, :])
    row_f = row8.astype(F32)
    decay = jnp.exp(-inv)
    for r in range(STEPS):
        powers[r * 8 : r * 8 + 8, :] = jnp.exp(-float(r + 1) * inv)
    joins = []
    for step in (1, 2, 4):
        power = jnp.exp(-float(12 * step) * inv)
        joins.append(
            (step, jnp.where(row8 >= step, power, 0.0), jnp.where(row8 < 8 - step, power, 0.0))
        )

    @pl.loop(0, 8)
    def _(j):
        values = [strided(mixed, j * COLS + r, 12, 768) for r in range(STEPS)]
        west = [None] * STEPS
        west[STEPS - 1] = values[STEPS - 1]
        for r in reversed(range(STEPS - 1)):
            west[r] = decay * west[r + 1] + values[r]
        east = values[0]
        field[tile(j * 13), :] = west[0]
        for r in range(1, STEPS):
            before = decay * east
            east = before + values[r]
            field[tile(j * 13 + r), :] = before + west[r]
        west = west[0]
        for step, up, down in joins:
            east = east + up * pltpu.roll(east, step, 0)
            west = west + down * pltpu.roll(west, 8 - step, 0)
        east_in[tile(j), :] = jnp.where(row8 >= 1, pltpu.roll(east, 1, 0), 0.0)
        west_in[tile(j), :] = jnp.where(row8 < 7, pltpu.roll(west, 7, 0), 0.0)
        lon_send[pl.ds(j, 1), :] = east[7:8, :]
        lon_send[pl.ds(8 + j, 1), :] = west[0:1, :]

    pl.semaphore_wait(barrier, 22)

    @pl.loop(1, 16)
    def _(i):
        pltpu.make_async_remote_copy(
            src_ref=lon_send,
            dst_ref=lon_recv.at[lon],
            send_sem=lon_sems.at[0],
            recv_sem=lon_sems.at[1],
            device_id=(lat, lax.rem(lon + i, 16)),
            device_id_type=MESH,
        ).start()

    for b in range(8):
        lengths[b] = table_ref[b : b + 1, :]

    for j in range(64):
        value = lengths[band_index_ref[j]]
        decays[j : j + 1, :] = value[:, :LANES]
        decays[64 + j : 65 + j, :] = value[:, LANES:]

    @pl.loop(0, 16)
    def _(r):
        value = jnp.exp(-1.0 / decays[tile(r), :])
        decays[tile(r), :] = value
        weights[tile(r), :] = jnp.sqrt(1.0 - value * value)

    for j in range(8):
        own_decay[j * 8 : j * 8 + 8, :] = wide(row_of(decays, first_row + j))
        own_weight[j * 8 : j * 8 + 8, :] = wide(row_of(weights, first_row + j))

    through = jnp.ones((8, WIDE), F32)
    answer = jnp.zeros((8, WIDE), F32)
    for j in reversed(range(8)):
        value = strided(decays, j, 8, 64)
        through = through * value
        answer = value * (strided(weights, j, 8, 64) + value * answer)
    small[0:8, :] = through
    squares = through * through
    for step in (1, 2, 4):
        there = row8 < 8 - step
        answer = answer + squares * jnp.where(there, pltpu.roll(answer, 8 - step, 0), 0.0)
        squares = squares * jnp.where(there, pltpu.roll(squares, 8 - step, 0), 0.0)
    small[8:16, :] = answer
    small[16:24, :] = jnp.zeros((8, WIDE), F32)

    def block_row(index):
        return small[pl.ds(index, 1), :]

    def chip_through(chip):
        first = jnp.clip(chip, 0, 3) * 2
        return block_row(first) * block_row(first + 1)

    own_through = wide(block_row(lat))
    partner_through = wide(block_row(z * 2 + 1 - core))
    reflection = wide(block_row(8 + lat + 1))
    outward = jnp.where(core == 1, -1, 1)
    second = chip_through(z + outward)
    third = second * chip_through(z + 2 * outward)
    chip_factors = [None, wide(second), wide(third)]

    owner = wide(table_ref[9:10, :])
    real_f = jnp.where(real, 1.0, 0.0)
    earlier = jnp.where(iota((WIDE, WIDE), 0) < iota((WIDE, WIDE), 1), 1.0, 0.0).astype(BF)
    device = iota((LANES, WIDE), 0).astype(F32)
    owned = jnp.where(
        (device == jnp.broadcast_to(table_ref[9:10, :], (LANES, WIDE)))
        & (jnp.broadcast_to(real_f[0:1, :], (LANES, WIDE)) > 0.5),
        1.0,
        0.0,
    )
    before = jnp.dot(owned.astype(BF), earlier, preferred_element_type=F32)
    rank = jnp.sum(owned * before, axis=0, keepdims=True)
    slot_of = jnp.where(real, owner * float(SLOTS) + wide(rank), -1.0).astype(jnp.int32)

    def place(o):
        oz, oc, oy, ox = o // 32, (o // 16) % 2, (o // 4) % 4, o % 4
        tlat = ((z + oz) & 3) * 2 + ((core + oc) & 1)
        tlon = ((y + oy) & 3) * 4 + ((x + ox) & 3)
        return tlat, tlon

    @pl.loop(0, 32)
    def _(r):
        row = iota((16, WIDE), 0) + r * 16
        o = ((row // SLOTS) * SPREAD) & 127
        oz, oc, oy, ox = o // 32, (o // 16) & 1, (o // 4) & 3, o & 3
        tlat = ((z + oz) & 3) * 2 + ((core + oc) & 1)
        tlon = ((y + oy) & 3) * 4 + ((x + ox) & 3)
        wanted = (tlat * 16 + tlon) * SLOTS + (row & 3)
        both = jnp.concatenate([slot_of, slot_of], axis=0)
        picks[pl.ds(pl.multiple_of(r * 16, 16), 16), :] = jnp.where(both == wanted, 1.0, 0.0).astype(BF)

    fifteen = lon_recv.at[pl.ds(0, 15)]
    pltpu.make_async_copy(fifteen, fifteen, lon_sems.at[1]).wait()

    block_power = [jnp.exp(-float(96 * n) * inv) for n in range(16)]
    closing = 1.0 / (1.0 - jnp.exp(-1536.0 * inv))
    east_total = lon_send[0:8, :] * block_power[15]
    west_total = lon_send[8:16, :] * block_power[15]
    for dq in range(1, 16):
        sender = lax.rem(lon + 16 - dq, 16)
        east_total = east_total + lon_recv[sender, 0:8, :] * block_power[dq - 1]
        west_total = west_total + lon_recv[sender, 8:16, :] * block_power[15 - dq]
    east_total = east_total * closing
    west_total = west_total * closing
    lon_total[0:8, :] = east_total
    lon_total[8:16, :] = west_total
    far_power = jnp.exp(-97.0 * inv)
    lon_total[16:24, :] = east_total + decay * lon_send[8:16, :] + far_power * west_total
    lon_total[24:32, :] = west_total + decay * lon_send[0:8, :] + far_power * east_total
    segment = jnp.exp(-12.0 * row_f * inv)
    segment_back = jnp.exp(-12.0 * (7.0 - row_f) * inv)
    for j in range(8):
        at = slice(j * 8, j * 8 + 8)
        east_in[at, :] = east_in[at, :] + wide(lon_total[j : j + 1, :]) * segment
        west_in[at, :] = west_in[at, :] + wide(lon_total[8 + j : 9 + j, :]) * segment_back
        beside = jnp.where(
            row8 == 0,
            wide(lon_total[16 + j : 17 + j, :]),
            jnp.where(row8 == 1, wide(lon_total[24 + j : 25 + j, :]), 0.0),
        )
        field[(j * 13 + 12) * 8 : (j * 13 + 13) * 8, :] = beside

    def chunk_rows(c):
        low, high = CHUNKS[c]
        return pl.ds(low * 8, (high - low) * 8)

    def exchange(src, dst, c, sems):
        return pltpu.make_async_remote_copy(
            src_ref=src.at[chunk_rows(c)],
            dst_ref=dst.at[chunk_rows(c)],
            send_sem=sems.at[0, c],
            recv_sem=sems.at[1, c],
            device_id=partner,
            device_id_type=MESH,
        )

    count = len(CHUNKS)
    near = [exchange(to_partner, near_recv, c, near_sems) for c in range(count)]
    far = [exchange(in_send, in_recv, c, far_sems) for c in range(count)]
    toward = jnp.where(core == 1, 1, -1)

    def chip_copy(c, d):
        target = z + toward * d
        return pltpu.make_async_remote_copy(
            src_ref=chip_send.at[chunk_rows(c)],
            dst_ref=chip_recv.at[d - 1, chunk_rows(c)],
            send_sem=chip_send_sems.at[c, d - 1],
            recv_sem=chip_recv_sems.at[c, d - 1],
            device_id=(target * 2 + core, lon),
            device_id_type=MESH,
        )

    def target_there(d):
        target = z + toward * d
        return (target >= 0) & (target < 4)

    def sender_there(d):
        sender = z - toward * d
        return (sender >= 0) & (sender < 4)

    def own(ref, j):
        return ref[j * 8 : j * 8 + 8, :]

    def edges(g, beside):
        north = jnp.zeros((8, WIDE), F32)
        values = []
        for j in range(8):
            value = field[tile(j * 13 + g), :]
            if not beside:
                value = (
                    value
                    + own(east_in, j) * powers[tile(g), :]
                    + own(west_in, j) * powers[tile(11 - g), :]
                )
                field[tile(j * 13 + g), :] = value
            north = own(own_decay, j) * north + own(own_weight, j) * value
            values.append(north)
        south = jnp.zeros((8, WIDE), F32)
        for j in reversed(range(8)):
            south = own(own_decay, j) * south + own(own_weight, j) * values[j]
        southbound = south + own_through * reflection * north
        north_end[tile(g), :] = north
        to_partner[tile(g), :] = jnp.where(core == 0, north, southbound)
        own_out[tile(g), :] = jnp.where(core == 0, southbound, north)

    for c in range(count):
        low, high = CHUNKS[c]

        @pl.loop(low, min(high, STEPS), unroll=2)
        def _(g):
            edges(g, False)

        if high > STEPS:
            edges(STEPS, True)
        near[c].start()

    for c in range(count):
        near[c].wait_recv()
        at = slice(CHUNKS[c][0] * 8, CHUNKS[c][1] * 8)
        for g in range(*CHUNKS[c]):
            at = slice(g * 8, g * 8 + 8)
            chip_send[at, :] = own_out[at, :] + own_through * near_recv[at, :]
        for d in range(1, 4):

            @pl.when(target_there(d))
            def _():
                chip_copy(c, d).start()

    for c in range(count):
        for d in range(1, 4):

            @pl.when(sender_there(d))
            def _():
                chip_copy(c, d).wait_recv()

        for g in range(*CHUNKS[c]):
            at = slice(g * 8, g * 8 + 8)
            total = jnp.where(sender_there(1), chip_recv[0, at, :], 0.0)
            for d in (2, 3):
                total = total + jnp.where(
                    sender_there(d), chip_factors[d - 1] * chip_recv[d - 1, at, :], 0.0
                )
            in_send[at, :] = total

        far[c].start()

    below_decay = wide(row_of(decays, jnp.maximum(first_row - 1, 0)))
    below_weight = wide(row_of(weights, jnp.maximum(first_row - 1, 0)))

    def finish(g, beside):
        at = tile(g)
        nearer = near_recv[at, :] + partner_through * in_send[at, :]
        farther = in_recv[at, :]
        north_in = jnp.where(core == 1, nearer, farther)
        south_sum = jnp.where(core == 1, farther, nearer)
        north_out = north_end[at, :] + own_through * north_in
        south_in = south_sum + reflection * north_out
        north = north_in
        values = []
        for j in range(8):
            north = own(own_decay, j) * north + own(own_weight, j) * field[tile(j * 13 + g), :]
            values.append(north)
        south = south_in
        results = [None] * 8 + [south_in]
        for j in reversed(range(8)):
            south = own(own_decay, j) * south + own(own_weight, j) * values[j]
            results[j] = south
        below = below_decay * results[0] + below_weight * north_in
        below = jnp.where(lat == 0, 0.0, below)
        for j in range(8):
            field[tile(j * 13 + g), :] = results[j]
            if not beside:
                lower = below if j == 0 else results[j - 1]
                slopes[tile(j * 12 + g), :] = (results[j + 1] - lower) * 0.5
                for t in range(2):
                    natural[pl.ds(t * 768 + j * COLS + g, 8, stride=12), :] = results[j][
                        :, t * LANES : t * LANES + LANES
                    ]

    for c in range(count):
        low, high = CHUNKS[c]
        far[c].wait_recv()

        @pl.loop(low, min(high, STEPS), unroll=2)
        def _(g):
            finish(g, False)

        if high > STEPS:
            finish(STEPS, True)

    quarter = x
    free = lane // 32 == 3 - quarter

    @pl.loop(0, 8)
    def _(j):
        for m in range(3):
            start = pl.multiple_of(j * COLS + m * 32, 32)
            high, low = split(
                jnp.concatenate([natural[pl.ds(start + t * 768, 32), :] for t in range(2)], axis=1)
            )
            at = pl.ds(pl.multiple_of(j * LANES + ((3 * quarter + m) & 3) * 32, 32), 32)
            turned_high[at, :] = high
            turned_low[at, :] = low
        at = pl.ds(pl.multiple_of(j * LANES + (3 - quarter) * 32, 32), 32)
        turned_high[at, :] = jnp.zeros((32, WIDE), BF)
        turned_low[at, :] = jnp.zeros((32, WIDE), BF)

    across = (((1,), (1,)), ((), ()))
    per_batch = 128 // BATCHES
    rows_batch = per_batch * SLOTS
    for b in range(BATCHES):
        chosen = picks[b * rows_batch : (b + 1) * rows_batch, :]
        for jp in range(4):
            at = slice(jp * WIDE, jp * WIDE + WIDE)
            out = lax.dot_general(
                chosen, turned_high[at, :], across, preferred_element_type=F32
            ) + lax.dot_general(chosen, turned_low[at, :], across, preferred_element_type=F32)
            for h in range(2):
                for q in range(rows_batch // 8):
                    by_slot[
                        pl.ds((b * rows_batch + q * 8) * 8 + jp * 2 + h, 8, stride=8), :
                    ] = out[q * 8 : q * 8 + 8, h * LANES : h * LANES + LANES]

        @pl.loop(b * per_batch, (b + 1) * per_batch, unroll=2)
        def _(u):
            last = by_slot[tile(u * SLOTS + 3), :]
            for i in range(3):
                extra = pltpu.roll(last, 32 * (3 - i), 1)
                blocks_out[u, :, i * LANES : (i + 1) * LANES] = jnp.where(
                    free, extra, by_slot[tile(u * SLOTS + i), :]
                )

        @pl.loop(max(b * per_batch, 1), (b + 1) * per_batch)
        def _(u):
            tlat, tlon = place((u * SPREAD) & 127)
            pltpu.make_async_remote_copy(
                src_ref=blocks_out.at[u],
                dst_ref=arrived_ref.at[me],
                send_sem=all_sems.at[0],
                recv_sem=all_sems.at[1],
                device_id=(tlat, tlon),
                device_id_type=MESH,
            ).start()

    kept = pltpu.make_async_copy(blocks_out.at[0], arrived_ref.at[me], all_sems.at[2])
    kept.start()

    latitude_row = (first_row + row8).astype(F32) + float(NLAT_GLOBE - 64)
    latitude = math.pi * ((latitude_row + 0.5) / NLAT_GLOBE - 0.5)
    metrics[...] = (0.5 / jnp.maximum(jnp.cos(latitude), 0.2))[:, :LANES]

    @pl.loop(0, 8)
    def _(j):
        metric = jnp.broadcast_to(metrics[pl.ds(j, 1), :], (8, LANES))
        beside = field[tile(j * 13 + 12), :]
        for g in range(STEPS):
            if g == STEPS - 1:
                after = jnp.where(
                    row8 == 7, wide(beside[1:2, :]), pltpu.roll(field[tile(j * 13), :], 7, 0)
                )
            else:
                after = field[tile(j * 13 + g + 1), :]
            if g == 0:
                ahead = jnp.where(
                    row8 == 0, wide(beside[0:1, :]), pltpu.roll(field[tile(j * 13 + 11), :], 1, 0)
                )
            else:
                ahead = field[tile(j * 13 + g - 1), :]
            along = after - ahead
            slope = slopes[tile(j * 12 + g), :]
            eastern = along[:, LANES:] * metric - slope[:, :LANES]
            northern = pltpu.roll(along[:, :LANES] * metric + slope[:, LANES:], LANES - 1, 1)
            at = j * COLS + g
            mixed[pl.ds(at, 8, stride=12), :] = jnp.where(lane < NLEV, eastern, northern)
            mixed[pl.ds(768 + at, 8, stride=12), :] = northern

    kept_winds = pltpu.make_async_copy(mixed, winds_ref, in_sem)
    kept_winds.start()

    pltpu.make_async_copy(fifteen, fifteen, lon_sems.at[0]).wait()
    for c in range(count):
        near[c].wait_send()
        far[c].wait_send()
        for d in range(1, 4):

            @pl.when(target_there(d))
            def _():
                chip_copy(c, d).wait_send()

    kept.wait()
    kept_winds.wait()
    others = blocks_out.at[pl.ds(0, 127)]
    landed = arrived_ref.at[pl.ds(0, 127)]
    pltpu.make_async_copy(others, others, all_sems.at[0]).wait()
    pltpu.make_async_copy(landed, landed, all_sems.at[1]).wait()


def slabs_kernel(arrived_ref, low_ref, high_ref, slabs_ref, winds_ref):
    lane = iota((8, LANES), 1)
    block = lane // 32
    for g in range(4):
        got = [
            [arrived_ref[4 * g + l, :, c * LANES : (c + 1) * LANES] for c in range(3)]
            for l in range(4)
        ]

        def put(slot, v, value):
            at = (g * 3 + v) * LANES
            slabs_ref[slot, :, at : at + LANES] = value

        moved = []
        for c in range(3):
            for v, width in enumerate((96, 64, 32)):
                put(c, v, jnp.where(lane < width, got[v][c], got[v + 1][c]))
            merged = jnp.where(
                block == 3,
                got[0][c],
                jnp.where(block == 2, got[1][c], jnp.where(block == 1, got[2][c], got[3][c])),
            )
            moved.append(pltpu.roll(merged, 32 * (c + 1), 1))
        for v in range(3):
            parts = [moved[(4 * v + b) % 3] for b in range(4)]
            value = jnp.where(
                block == 0,
                parts[0],
                jnp.where(block == 1, parts[1], jnp.where(block == 2, parts[2], parts[3])),
            )
            put(3, v, value)
    winds_ref[0, :, 0:LANES] = low_ref[...]
    winds_ref[0, :, LANES : 2 * NLEV] = high_ref[:, 0 : 2 * NLEV - LANES]


def padded_rows(rows, fill):
    pairs = rows.reshape(rows.shape[0], 2, NLEV)
    return jnp.pad(pairs, ((0, 0), (0, 0), (0, 1)), constant_values=fill).reshape(-1, WIDE)


def shards(control, vert_band, lat_length, lon_length, band_index, owner_device):
    rows = jnp.concatenate(
        [lat_length.T, lon_length[None, :], owner_device.T.astype(F32)], axis=0
    )
    table = jnp.concatenate(
        [
            jnp.pad(padded_rows(rows, 1.0), ((0, 6), (0, 0))),
            jnp.pad(
                jnp.pad(vert_band.transpose(1, 0, 2), ((0, 0), (0, 0), (0, 1))).reshape(9, WIDE),
                ((0, 7), (0, 0)),
            ),
        ],
        axis=0,
    )
    vmem = pltpu.VMEM
    edge = vmem((HIGH, WIDE), F32)
    dma = pltpu.SemaphoreType.DMA
    count = len(CHUNKS)
    arrived, winds_wide = pl.pallas_call(
        columns_kernel,
        out_shape=(
            jax.ShapeDtypeStruct((128, 8, 3 * LANES), F32),
            jax.ShapeDtypeStruct((16 * COLS, LANES), F32),
        ),
        in_specs=[
            pl.BlockSpec(memory_space=pltpu.SMEM),
            pl.BlockSpec(memory_space=vmem),
            pl.BlockSpec(memory_space=pl.ANY),
        ],
        out_specs=(pl.BlockSpec(memory_space=pl.ANY), pl.BlockSpec(memory_space=pl.ANY)),
        scratch_shapes=[
            vmem((8, COLS, 2 * NLEV), F32),
            vmem((8 * COLS, WIDE), BF),
            vmem((8 * COLS, WIDE), BF),
            vmem((WIDE, WIDE), BF),
            vmem((WIDE, WIDE), BF),
            vmem((16 * COLS, LANES), F32),
            vmem((8 * HIGH, WIDE), F32),
            vmem((8 * COLS, WIDE), F32),
            vmem((16 * COLS, LANES), F32),
            vmem((8 * LANES, WIDE), BF),
            vmem((8 * LANES, WIDE), BF),
            vmem((512, WIDE), BF),
            vmem((4096, LANES), F32),
            vmem((128, 8, 3 * LANES), F32),
            vmem((8, 1, WIDE), F32),
            vmem((128, LANES), F32),
            vmem((128, LANES), F32),
            vmem((64, WIDE), F32),
            vmem((64, WIDE), F32),
            vmem((32, WIDE), F32),
            vmem((8, LANES), F32),
            vmem((COLS, WIDE), F32),
            vmem((64, WIDE), F32),
            vmem((64, WIDE), F32),
            vmem((16, WIDE), F32),
            vmem((16, 16, WIDE), F32),
            vmem((32, WIDE), F32),
            edge,
            edge,
            edge,
            edge,
            vmem((3, HIGH, WIDE), F32),
            edge,
            edge,
            edge,
            dma,
            dma((2,)),
            dma((2, count)),
            dma((count, 3)),
            dma((count, 3)),
            dma((2, count)),
            dma((3,)),
        ],
        compiler_params=pltpu.CompilerParams(collective_id=0, has_side_effects=True),
        name="columns",
    )(band_index, table, control.transpose(1, 2, 0))
    slabs, winds = pl.pallas_call(
        slabs_kernel,
        grid=(8,),
        out_shape=(
            jax.ShapeDtypeStruct((SLOTS, 64, 1536), F32),
            jax.ShapeDtypeStruct((8, COLS, 2 * NLEV), F32),
        ),
        in_specs=[
            pl.BlockSpec((16, 8, 3 * LANES), lambda i: (i, 0, 0)),
            pl.BlockSpec((COLS, LANES), lambda i: (i, 0)),
            pl.BlockSpec((COLS, LANES), lambda i: (8 + i, 0)),
        ],
        out_specs=(
            pl.BlockSpec((SLOTS, 8, 1536), lambda i: (0, i, 0)),
            pl.BlockSpec((1, COLS, 2 * NLEV), lambda i: (i, 0, 0)),
        ),
        name="slabs",
    )(arrived, winds_wide, winds_wide)
    return (winds.transpose(2, 0, 1), slabs)


def solution(mesh):
    placed = (P(None, "lat", "lon"), P(), P(), P(), P(), P())
    return jax.shard_map(
        shards,
        mesh=mesh,
        in_specs=placed,
        out_specs=(P(None, "lat", "lon"), P(("lat", "lon"), None, None)),
        check_vma=False,
    )
```

time: 140 us -> 57.4 us (0.41)
  Pallas kernels: 128 us -> 52.6 us
  local copies, waits for them, and re-layouts: 6.33 us -> 2.35 us
  other arithmetic: 4.5 us -> 1.33 us
    pallas_call x1, Pallas kernels: 122 us -> 46.7 us  [shards(): pl.pallas_call(columns_kernel, out_shape=(jax.ShapeDtypeStruct((128, 8, 3...]
    unnamed x3 -> x4, local copies, waits for them, and re-layouts: 6.21 us -> 0.02 us
    concatenate x1 -> x2, local copies, waits for them, and re-layouts: 0.12 us -> 1.53 us  [shards(): jnp.concatenate([lat_length.T, lon_length[None, :], owner_device.T.astype...]
where the time goes in v2:
time: 57.4 us; the launch traced here: 57 us
  Pallas kernels  52.6 us (92%)
  local copies, waits for them, and re-layouts  2.35 us (4%)
  other arithmetic  1.33 us (2%)
  between operations  0.67 us (1%)
    pallas_call x1, Pallas kernels, shards(): pl.pallas_call(columns_kernel, out_shape=(jax.ShapeDtypeStruct((128, 8, 3...  46.7 us
    pallas_call x1, Pallas kernels, shards(): pl.pallas_call(slabs_kernel, grid=(8,), out_shape=(jax.ShapeDtypeStruct((...  5.9 us
    concatenate x2, local copies, waits for them, and re-layouts, shards(): jnp.concatenate([lat_length.T, lon_length[None, :], owner_device.T.astype...  1.53 us

profile of v2, /device:TPU:1, one launch (start us, length us, event | category | flops | bytes accessed | tf_op | source)
XLA Modules:
  0.0 57.0 jit_solution(9053863679524803346)
XLA Ops:
  0.6 0.8 %concatenate.12 = f32[1,2,127]{2,1,0:T(2,128)S(1)} reshape(f32[254]{0:T(256)} %param.9) | data formatting | bytes 2032 | tf_op jit(solution)/shard_map/concatenate | solution.py:632
  1.4 0.7 %convert_reduce_fusion = f32[254]{0:T(256)S(1)} fusion(s32[254,1]{0,1:T(1,128)} %param.11), kind=kLoop, calls=%fused_computation.5 | loop fusion | flops 254 | bytes 2032 | tf_op jit(solution)/shard_map/convert_element_type | solution.py:633
  2.1 0.1 convert_element_type.22
  2.2 0.8 %concatenate.11 = f32[8,2,127]{2,1,0:T(2,128)S(1)} reshape(f32[8,254]{1,0:T(8,128)} %bitcast.16) | data formatting | bytes 16256 | tf_op jit(solution)/shard_map/concatenate | solution.py:632
  3.0 0.7 %pad.18 = f32[9,2,128]{2,1,0:T(2,128)S(1)} pad(f32[9,2,127]{2,1,0:T(2,128)} %bitcast.15, f32[]{:T(128)} %constant.4.clone.1), padding=0_0x0_0x0_1 | pad | bytes 18364 | tf_op jit(solution)/shard_map/jit(_pad)/pad | solution.py:639
  3.7 0.6 %select_maximum_fusion.table_ref = f32[32,256]{1,0:T(8,128)} fusion(f32[9,256]{1,0:T(8,128)S(1)} %bitcast.14, f32[10,256]{1,0:T(8,128)S(1)} %bitcast.13), kind=kLoop, calls=%fused_computation | loop fusion | flops 40960 | bytes 52224 | tf_op jit(solution)/shard_map/concatenate | solution.py:635
  4.3 46.7 %columns.1 = (f32[128,8,384]{2,1,0:T(8,128)}, f32[1536,128]{1,0:T(8,128)}) custom-call(s32[64]{0:T(128)} %band_index_ref.1, f32[32,256]{1,0:T(8,128)} %select_maximum_fusion.table_ref, f32[8,96,254]{2,1,0:T(8,128)} %bitcast.10), custom_call_target="tpu_custom_call" | custom-call | tf_op jit(solution)/shard_map/columns/pallas_call | solution.py:649
  51.1 5.9 %slabs.1 = (f32[4,64,1536]{2,1,0:T(8,128)}, f32[8,96,254]{2,1,0:T(8,128)}) custom-call(f32[128,8,384]{2,1,0:T(8,128)} %get-tuple-element.6.arrived_ref, f32[1536,128]{1,0:T(8,128)} %get-tuple-element.7.low_ref.high_ref, f32[1536,128]{1,0:T(8,128)} %get-tuple-element.7.low_ref.high_ref), custom_call_target="tpu_custom_call" | custom-call | tf_op jit(solution)/shard_map/slabs/pallas_call | solution.py:708
  (5 shorter events, 0.0 us)

commit v3 on v2

--- a/solution.py
+++ b/solution.py
@@ -19,6 +19,7 @@
 CHUNKS = ((0, 6), (6, 13))
 BATCHES = 2
 SPREAD = 45
+LATS = 4
 BF = jnp.bfloat16
 F32 = jnp.float32
 
@@ -52,11 +53,19 @@
 
 def columns_kernel(
     band_index_ref,
-    table_ref,
+    lat_ref,
+    lon_ref,
+    band_ref,
+    owner_ref,
     control_ref,
     arrived_ref,
     winds_ref,
     control_in,
+    lat_in,
+    lon_in,
+    band_in,
+    owner_in,
+    table_ref,
     parts_high,
     parts_low,
     band_high,
@@ -83,6 +92,12 @@
     lon_send,
     lon_recv,
     lon_total,
+    sides,
+    side_send,
+    side_recv,
+    east_all,
+    west_all,
+    beside_all,
     to_partner,
     own_out,
     near_recv,
@@ -92,7 +107,9 @@
     in_recv,
     north_end,
     in_sem,
+    raw_sems,
     lon_sems,
+    side_sems,
     near_sems,
     chip_send_sems,
     chip_recv_sems,
@@ -123,9 +140,33 @@
 
     load = pltpu.make_async_copy(control_ref, control_in, in_sem)
     load.start()
+    raw = [
+        pltpu.make_async_copy(src, dst, raw_sems.at[i])
+        for i, (src, dst) in enumerate(
+            ((lat_ref, lat_in), (lon_ref, lon_in), (band_ref, band_in), (owner_ref, owner_in))
+        )
+    ]
+    for copy in raw:
+        copy.start()
 
     row8 = iota((8, WIDE), 0)
     lane = iota((8, LANES), 1)
+
+    for copy in raw:
+        copy.wait()
+    table_ref[...] = jnp.ones((32, WIDE), F32)
+    table_ref[0:8, 0 : 2 * NLEV] = lat_in[...]
+    table_ref[8:9, 0 : 2 * NLEV] = lon_in[...]
+    table_ref[9:10, 0 : 2 * NLEV] = owner_in[...].astype(F32)
+    for h in range(2):
+        at = slice(h * 8, h * 8 + 8)
+        first, second = table_ref[at, 0:LANES], table_ref[at, LANES:WIDE]
+        moved = jnp.where(lane == 0, pltpu.roll(first, 1, 1), pltpu.roll(second, 1, 1))
+        table_ref[at, 0:LANES] = jnp.where(lane < NLEV, first, 1.0)
+        table_ref[at, LANES:WIDE] = jnp.where(lane < NLEV, moved, 1.0)
+    for o in range(9):
+        table_ref[16 + o : 17 + o, 0:NLEV] = band_in[o, 0:1, :]
+        table_ref[16 + o : 17 + o, LANES : LANES + NLEV] = band_in[o, 1:2, :]
 
     column = iota((8, WIDE), 1)
     kind = column // LANES
@@ -210,19 +251,6 @@
         lon_send[pl.ds(j, 1), :] = east[7:8, :]
         lon_send[pl.ds(8 + j, 1), :] = west[0:1, :]
 
-    pl.semaphore_wait(barrier, 22)
-
-    @pl.loop(1, 16)
-    def _(i):
-        pltpu.make_async_remote_copy(
-            src_ref=lon_send,
-            dst_ref=lon_recv.at[lon],
-            send_sem=lon_sems.at[0],
-            recv_sem=lon_sems.at[1],
-            device_id=(lat, lax.rem(lon + i, 16)),
-            device_id_type=MESH,
-        ).start()
-
     for b in range(8):
         lengths[b] = table_ref[b : b + 1, :]
 
@@ -271,6 +299,154 @@
     third = second * chip_through(z + 2 * outward)
     chip_factors = [None, wide(second), wide(third)]
 
+    for j in range(8):
+        field[(j * 13 + 12) * 8 : (j * 13 + 13) * 8, :] = decay * jnp.where(
+            row8 == 0,
+            wide(lon_send[8 + j : 9 + j, :]),
+            jnp.where(row8 == 1, wide(lon_send[j : j + 1, :]), 0.0),
+        )
+
+    def chunk_rows(c):
+        low, high = CHUNKS[c]
+        return pl.ds(low * 8, (high - low) * 8)
+
+    def exchange(src, dst, c, sems):
+        return pltpu.make_async_remote_copy(
+            src_ref=src.at[chunk_rows(c)],
+            dst_ref=dst.at[chunk_rows(c)],
+            send_sem=sems.at[0, c],
+            recv_sem=sems.at[1, c],
+            device_id=partner,
+            device_id_type=MESH,
+        )
+
+    count = len(CHUNKS)
+    near = [exchange(to_partner, near_recv, c, near_sems) for c in range(count)]
+    far = [exchange(in_send, in_recv, c, far_sems) for c in range(count)]
+    toward = jnp.where(core == 1, 1, -1)
+
+    def chip_copy(c, d):
+        target = z + toward * d
+        return pltpu.make_async_remote_copy(
+            src_ref=chip_send.at[chunk_rows(c)],
+            dst_ref=chip_recv.at[d - 1, chunk_rows(c)],
+            send_sem=chip_send_sems.at[c, d - 1],
+            recv_sem=chip_recv_sems.at[c, d - 1],
+            device_id=(target * 2 + core, lon),
+            device_id_type=MESH,
+        )
+
+    def target_there(d):
+        target = z + toward * d
+        return (target >= 0) & (target < 4)
+
+    def sender_there(d):
+        sender = z - toward * d
+        return (sender >= 0) & (sender < 4)
+
+    def own(ref, j):
+        return ref[j * 8 : j * 8 + 8, :]
+
+    side = None
+
+    def edges(g, beside):
+        north = jnp.zeros((8, WIDE), F32)
+        values = []
+        for j in range(8):
+            value = sides[tile(j), :] if g is side else field[tile(j * 13 + g), :]
+            if not beside:
+                value = (
+                    value
+                    + own(east_in, j) * powers[tile(g), :]
+                    + own(west_in, j) * powers[tile(11 - g), :]
+                )
+                field[tile(j * 13 + g), :] = value
+            north = own(own_decay, j) * north + own(own_weight, j) * value
+            values.append(north)
+        south = jnp.zeros((8, WIDE), F32)
+        for j in reversed(range(8)):
+            south = own(own_decay, j) * south + own(own_weight, j) * values[j]
+        southbound = south + own_through * reflection * north
+        if g is side:
+            return north, southbound
+        north_end[tile(g), :] = north
+        to_partner[tile(g), :] = jnp.where(core == 0, north, southbound)
+        own_out[tile(g), :] = jnp.where(core == 0, southbound, north)
+
+    for c in range(count):
+        low, high = CHUNKS[c]
+
+        @pl.loop(low, min(high, STEPS), unroll=2)
+        def _(g):
+            edges(g, False)
+
+        if high > STEPS:
+            edges(STEPS, True)
+
+    pl.semaphore_wait(barrier, 22)
+
+    @pl.loop(1, 16)
+    def _(i):
+        pltpu.make_async_remote_copy(
+            src_ref=lon_send,
+            dst_ref=lon_recv.at[lon],
+            send_sem=lon_sems.at[0],
+            recv_sem=lon_sems.at[1],
+            device_id=(lat, lax.rem(lon + i, 16)),
+            device_id_type=MESH,
+        ).start()
+
+    for c in range(count):
+        near[c].start()
+
+    for c in range(count):
+        near[c].wait_recv()
+        at = slice(CHUNKS[c][0] * 8, CHUNKS[c][1] * 8)
+        for g in range(*CHUNKS[c]):
+            at = slice(g * 8, g * 8 + 8)
+            chip_send[at, :] = own_out[at, :] + own_through * near_recv[at, :]
+        for d in range(1, 4):
+
+            @pl.when(target_there(d))
+            def _():
+                chip_copy(c, d).start()
+
+    fifteen = lon_recv.at[pl.ds(0, 15)]
+    pltpu.make_async_copy(fifteen, fifteen, lon_sems.at[1]).wait()
+
+    block_power = [jnp.exp(-float(96 * n) * inv) for n in range(16)]
+    closing = 1.0 / (1.0 - jnp.exp(-1536.0 * inv))
+    east_total = lon_send[0:8, :] * block_power[15]
+    west_total = lon_send[8:16, :] * block_power[15]
+    for dq in range(1, 16):
+        sender = lax.rem(lon + 16 - dq, 16)
+        east_total = east_total + lon_recv[sender, 0:8, :] * block_power[dq - 1]
+        west_total = west_total + lon_recv[sender, 8:16, :] * block_power[15 - dq]
+    east_total = east_total * closing
+    west_total = west_total * closing
+
+    lon_total[0:8, :] = east_total
+    lon_total[8:16, :] = west_total
+    for j in range(8):
+        sides[j * 8 : j * 8 + 8, :] = jnp.where(
+            row8 == 0,
+            wide(lon_total[j : j + 1, :]),
+            jnp.where(row8 == 1, wide(lon_total[8 + j : 9 + j, :]), 0.0),
+        )
+    side_north, side_south = edges(side, True)
+    side_send[...] = jnp.where(row8 < 2, side_north, pltpu.roll(side_south, 2, 0))
+
+    @pl.loop(1, 8)
+    def _(i):
+        pltpu.make_async_remote_copy(
+            src_ref=side_send,
+            dst_ref=side_recv.at[lat],
+            send_sem=side_sems.at[0],
+            recv_sem=side_sems.at[1],
+            device_id=(lax.rem(lat + i, 8), lon),
+            device_id_type=MESH,
+        ).start()
+
     owner = wide(table_ref[9:10, :])
     real_f = jnp.where(real, 1.0, 0.0)
     earlier = jnp.where(iota((WIDE, WIDE), 0) < iota((WIDE, WIDE), 1), 1.0, 0.0).astype(BF)
@@ -302,123 +478,6 @@
         both = jnp.concatenate([slot_of, slot_of], axis=0)
         picks[pl.ds(pl.multiple_of(r * 16, 16), 16), :] = jnp.where(both == wanted, 1.0, 0.0).astype(BF)
 
-    fifteen = lon_recv.at[pl.ds(0, 15)]
-    pltpu.make_async_copy(fifteen, fifteen, lon_sems.at[1]).wait()
-
-    block_power = [jnp.exp(-float(96 * n) * inv) for n in range(16)]
-    closing = 1.0 / (1.0 - jnp.exp(-1536.0 * inv))
-    east_total = lon_send[0:8, :] * block_power[15]
-    west_total = lon_send[8:16, :] * block_power[15]
-    for dq in range(1, 16):
-        sender = lax.rem(lon + 16 - dq, 16)
-        east_total = east_total + lon_recv[sender, 0:8, :] * block_power[dq - 1]
-        west_total = west_total + lon_recv[sender, 8:16, :] * block_power[15 - dq]
-    east_total = east_total * closing
-    west_total = west_total * closing
-    lon_total[0:8, :] = east_total
-    lon_total[8:16, :] = west_total
-    far_power = jnp.exp(-97.0 * inv)
-    lon_total[16:24, :] = east_total + decay * lon_send[8:16, :] + far_power * west_total
-    lon_total[24:32, :] = west_total + decay * lon_send[0:8, :] + far_power * east_total
-    segment = jnp.exp(-12.0 * row_f * inv)
-    segment_back = jnp.exp(-12.0 * (7.0 - row_f) * inv)
-    for j in range(8):
-        at = slice(j * 8, j * 8 + 8)
-        east_in[at, :] = east_in[at, :] + wide(lon_total[j : j + 1, :]) * segment
-        west_in[at, :] = west_in[at, :] + wide(lon_total[8 + j : 9 + j, :]) * segment_back
-        beside = jnp.where(
-            row8 == 0,
-            wide(lon_total[16 + j : 17 + j, :]),
-            jnp.where(row8 == 1, wide(lon_total[24 + j : 25 + j, :]), 0.0),
-        )
-        field[(j * 13 + 12) * 8 : (j * 13 + 13) * 8, :] = beside
-
-    def chunk_rows(c):
-        low, high = CHUNKS[c]
-        return pl.ds(low * 8, (high - low) * 8)
-
-    def exchange(src, dst, c, sems):
-        return pltpu.make_async_remote_copy(
-            src_ref=src.at[chunk_rows(c)],
-            dst_ref=dst.at[chunk_rows(c)],
-            send_sem=sems.at[0, c],
-            recv_sem=sems.at[1, c],
-            device_id=partner,
-            device_id_type=MESH,
-        )
-
-    count = len(CHUNKS)
-    near = [exchange(to_partner, near_recv, c, near_sems) for c in range(count)]
-    far = [exchange(in_send, in_recv, c, far_sems) for c in range(count)]
-    toward = jnp.where(core == 1, 1, -1)
-
-    def chip_copy(c, d):
-        target = z + toward * d
-        return pltpu.make_async_remote_copy(
-            src_ref=chip_send.at[chunk_rows(c)],
-            dst_ref=chip_recv.at[d - 1, chunk_rows(c)],
-            send_sem=chip_send_sems.at[c, d - 1],
-            recv_sem=chip_recv_sems.at[c, d - 1],
-            device_id=(target * 2 + core, lon),
-            device_id_type=MESH,
-        )
-
-    def target_there(d):
-        target = z + toward * d
-        return (target >= 0) & (target < 4)
-
-    def sender_there(d):
-        sender = z - toward * d
-        return (sender >= 0) & (sender < 4)
-
-    def own(ref, j):
-        return ref[j * 8 : j * 8 + 8, :]
-
-    def edges(g, beside):
-        north = jnp.zeros((8, WIDE), F32)
-        values = []
-        for j in range(8):
-            value = field[tile(j * 13 + g), :]
-            if not beside:
-                value = (
-                    value
-                    + own(east_in, j) * powers[tile(g), :]
-                    + own(west_in, j) * powers[tile(11 - g), :]
-                )
-                field[tile(j * 13 + g), :] = value
-            north = own(own_decay, j) * north + own(own_weight, j) * value
-            values.append(north)
-        south = jnp.zeros((8, WIDE), F32)
-        for j in reversed(range(8)):
-            south = own(own_decay, j) * south + own(own_weight, j) * values[j]
-        southbound = south + own_through * reflection * north
-        north_end[tile(g), :] = north
-        to_partner[tile(g), :] = jnp.where(core == 0, north, southbound)
-        own_out[tile(g), :] = jnp.where(core == 0, southbound, north)
-
-    for c in range(count):
-        low, high = CHUNKS[c]
-
-        @pl.loop(low, min(high, STEPS), unroll=2)
-        def _(g):
-            edges(g, False)
-
-        if high > STEPS:
-            edges(STEPS, True)
-        near[c].start()
-
-    for c in range(count):
-        near[c].wait_recv()
-        at = slice(CHUNKS[c][0] * 8, CHUNKS[c][1] * 8)
-        for g in range(*CHUNKS[c]):
-            at = slice(g * 8, g * 8 + 8)
-            chip_send[at, :] = own_out[at, :] + own_through * near_recv[at, :]
-        for d in range(1, 4):
-
-            @pl.when(target_there(d))
-            def _():
-                chip_copy(c, d).start()
-
     for c in range(count):
         for d in range(1, 4):
 
@@ -439,6 +498,44 @@
 
     below_decay = wide(row_of(decays, jnp.maximum(first_row - 1, 0)))
     below_weight = wide(row_of(weights, jnp.maximum(first_row - 1, 0)))
+
+    seven = side_recv.at[pl.ds(0, 7)]
+    pltpu.make_async_copy(seven, seven, side_sems.at[1]).wait()
+    side_in = jnp.zeros((8, WIDE), F32)
+    for p in range(7):
+        side_in = jnp.where(p < lat, wide(small[p : p + 1, :]) * side_in + side_recv[p], side_in)
+    side_back = jnp.zeros((8, WIDE), F32)
+    for p in reversed(range(1, 8)):
+        side_back = jnp.where(
+            p > lat, wide(small[p : p + 1, :]) * side_back + side_recv[p], side_back
+        )
+    side_back = pltpu.roll(side_back, 6, 0) + reflection * (side_north + own_through * side_in)
+    north = side_in
+    values = []
+    for j in range(8):
+        north = own(own_decay, j) * north + own(own_weight, j) * own(sides, j)
+        values.append(north)
+    south = side_back
+    rows = [None] * 8 + [side_back]
+    for j in reversed(range(8)):
+        south = own(own_decay, j) * south + own(own_weight, j) * values[j]
+        rows[j] = south
+    edge_row = below_decay * rows[0] + below_weight * side_in
+    rows = [jnp.where(lat == 0, 0.0, edge_row)] + rows
+    far_power = jnp.exp(-97.0 * inv)
+    segment = jnp.exp(-12.0 * row_f * inv)
+    segment_back = jnp.exp(-12.0 * (7.0 - row_f) * inv)
+    east_beside = jnp.where(row8 == 0, 1.0, far_power)
+    west_beside = jnp.where(row8 == 0, far_power, 1.0)
+    for j in range(10):
+        at = slice(j * 8, j * 8 + 8)
+        from_west, from_east = wide(rows[j][0:1, :]), wide(rows[j][1:2, :])
+        east_all[at, :] = from_west * segment
+        west_all[at, :] = from_east * segment_back
+        if 1 <= j <= 8:
+            beside_all[(j - 1) * 8 : j * 8, :] = (
+                from_west * east_beside + from_east * west_beside
+            )
 
     def finish(g, beside):
         at = tile(g)
@@ -460,6 +557,16 @@
             results[j] = south
         below = below_decay * results[0] + below_weight * north_in
         below = jnp.where(lat == 0, 0.0, below)
+        if beside:
+            for j in range(8):
+                field[tile(j * 13 + g), :] = results[j] + own(beside_all, j)
+            return
+        toward_east, toward_west = powers[tile(g), :], powers[tile(11 - g), :]
+        results = [
+            value + own(east_all, j) * toward_east + own(west_all, j) * toward_west
+            for j, value in enumerate([below] + results)
+        ]
+        below, results = results[0], results[1:]
         for j in range(8):
             field[tile(j * 13 + g), :] = results[j]
             if not beside:
@@ -571,6 +678,7 @@
     kept_winds.start()
 
     pltpu.make_async_copy(fifteen, fifteen, lon_sems.at[0]).wait()
+    pltpu.make_async_copy(seven, seven, side_sems.at[0]).wait()
     for c in range(count):
         near[c].wait_send()
         far[c].wait_send()
@@ -591,15 +699,15 @@
 def slabs_kernel(arrived_ref, low_ref, high_ref, slabs_ref, winds_ref):
     lane = iota((8, LANES), 1)
     block = lane // 32
-    for g in range(4):
+    for q, g in [(q, g) for q in range(LATS) for g in range(4)]:
         got = [
-            [arrived_ref[4 * g + l, :, c * LANES : (c + 1) * LANES] for c in range(3)]
+            [arrived_ref[16 * q + 4 * g + l, :, c * LANES : (c + 1) * LANES] for c in range(3)]
             for l in range(4)
         ]
 
         def put(slot, v, value):
             at = (g * 3 + v) * LANES
-            slabs_ref[slot, :, at : at + LANES] = value
+            slabs_ref[slot, 8 * q : 8 * q + 8, at : at + LANES] = value
 
         moved = []
         for c in range(3):
@@ -619,29 +727,12 @@
                 jnp.where(block == 1, parts[1], jnp.where(block == 2, parts[2], parts[3])),
             )
             put(3, v, value)
-    winds_ref[0, :, 0:LANES] = low_ref[...]
-    winds_ref[0, :, LANES : 2 * NLEV] = high_ref[:, 0 : 2 * NLEV - LANES]
-
-
-def padded_rows(rows, fill):
-    pairs = rows.reshape(rows.shape[0], 2, NLEV)
-    return jnp.pad(pairs, ((0, 0), (0, 0), (0, 1)), constant_values=fill).reshape(-1, WIDE)
+    for q in range(LATS):
+        winds_ref[q, :, 0:LANES] = low_ref[q * COLS : (q + 1) * COLS, :]
+        winds_ref[q, :, LANES : 2 * NLEV] = high_ref[q * COLS : (q + 1) * COLS, 0 : 2 * NLEV - LANES]
 
 
 def shards(control, vert_band, lat_length, lon_length, band_index, owner_device):
-    rows = jnp.concatenate(
-        [lat_length.T, lon_length[None, :], owner_device.T.astype(F32)], axis=0
-    )
-    table = jnp.concatenate(
-        [
-            jnp.pad(padded_rows(rows, 1.0), ((0, 6), (0, 0))),
-            jnp.pad(
-                jnp.pad(vert_band.transpose(1, 0, 2), ((0, 0), (0, 0), (0, 1))).reshape(9, WIDE),
-                ((0, 7), (0, 0)),
-            ),
-        ],
-        axis=0,
-    )
     vmem = pltpu.VMEM
     edge = vmem((HIGH, WIDE), F32)
     dma = pltpu.SemaphoreType.DMA
@@ -654,12 +745,16 @@
         ),
         in_specs=[
             pl.BlockSpec(memory_space=pltpu.SMEM),
-            pl.BlockSpec(memory_space=vmem),
-            pl.BlockSpec(memory_space=pl.ANY),
-        ],
+        ]
+        + [pl.BlockSpec(memory_space=pl.ANY)] * 5,
         out_specs=(pl.BlockSpec(memory_space=pl.ANY), pl.BlockSpec(memory_space=pl.ANY)),
         scratch_shapes=[
             vmem((8, COLS, 2 * NLEV), F32),
+            vmem((8, 2 * NLEV), F32),
+            vmem((1, 2 * NLEV), F32),
+            vmem((9, 2, NLEV), F32),
+            vmem((1, 2 * NLEV), jnp.int32),
+            vmem((32, WIDE), F32),
             vmem((8 * COLS, WIDE), BF),
             vmem((8 * COLS, WIDE), BF),
             vmem((WIDE, WIDE), BF),
@@ -686,6 +781,12 @@
             vmem((16, WIDE), F32),
             vmem((16, 16, WIDE), F32),
             vmem((32, WIDE), F32),
+            vmem((64, WIDE), F32),
+            vmem((8, WIDE), F32),
+            vmem((8, 8, WIDE), F32),
+            vmem((80, WIDE), F32),
+            vmem((80, WIDE), F32),
+            vmem((64, WIDE), F32),
             edge,
             edge,
             edge,
@@ -695,6 +796,8 @@
             edge,
             edge,
             dma,
+            dma((4,)),
+            dma((2,)),
             dma((2,)),
             dma((2, count)),
             dma((count, 3)),
@@ -704,22 +807,29 @@
         ],
         compiler_params=pltpu.CompilerParams(collective_id=0, has_side_effects=True),
         name="columns",
-    )(band_index, table, control.transpose(1, 2, 0))
+    )(
+        band_index,
+        lat_length.T,
+        lon_length[None, :],
+        vert_band.transpose(1, 0, 2),
+        owner_device.T,
+        control.transpose(1, 2, 0),
+    )
     slabs, winds = pl.pallas_call(
         slabs_kernel,
-        grid=(8,),
+        grid=(8 // LATS,),
         out_shape=(
             jax.ShapeDtypeStruct((SLOTS, 64, 1536), F32),
             jax.ShapeDtypeStruct((8, COLS, 2 * NLEV), F32),
         ),
         in_specs=[
-            pl.BlockSpec((16, 8, 3 * LANES), lambda i: (i, 0, 0)),
-            pl.BlockSpec((COLS, LANES), lambda i: (i, 0)),
-            pl.BlockSpec((COLS, LANES), lambda i: (8 + i, 0)),
+            pl.BlockSpec((16 * LATS, 8, 3 * LANES), lambda i: (i, 0, 0)),
+            pl.BlockSpec((COLS * LATS, LANES), lambda i: (i, 0)),
+            pl.BlockSpec((COLS * LATS, LANES), lambda i: (8 // LATS + i, 0)),
         ],
         out_specs=(
-            pl.BlockSpec((SLOTS, 8, 1536), lambda i: (0, i, 0)),
-            pl.BlockSpec((1, COLS, 2 * NLEV), lambda i: (i, 0, 0)),
+            pl.BlockSpec((SLOTS, 8 * LATS, 1536), lambda i: (0, i, 0)),
+            pl.BlockSpec((LATS, COLS, 2 * NLEV), lambda i: (i, 0, 0)),
         ),
         name="slabs",
     )(arrived, winds_wide, winds_wide)

time: 57.4 us -> 48.1 us (0.84)
  Pallas kernels: 52.6 us -> 47.3 us
  local copies, waits for them, and re-layouts: 2.35 us -> 0 us
  other arithmetic: 1.33 us -> 0 us
    pallas_call x1, Pallas kernels: 5.9 us -> 2.84 us  [shards(): pl.pallas_call(slabs_kernel, grid=(8 // LATS,), out_shape=(jax.ShapeDtype...]
    pallas_call x1, Pallas kernels: 46.7 us -> 44.5 us  [shards(): pl.pallas_call(columns_kernel, out_shape=(jax.ShapeDtypeStruct((128, 8, 3...]
    concatenate x2 -> x0, local copies, waits for them, and re-layouts: 1.53 us -> none  [shards(): jnp.concatenate([lat_length.T, lon_length[None, :], owner_device.T.astype...]
    pad x1 -> x0, local copies, waits for them, and re-layouts: 0.71 us -> none  [shards(): jnp.pad(vert_band.transpose(1, 0, 2), ((0, 0), (0, 0), (0, 1)))]
    convert_element_type x1 -> x0, other arithmetic: 0.7 us -> none  [shards(): owner_device.T.astype(F32)]
    concatenate x2 -> x0, other arithmetic: 0.63 us -> none  [the longest x1 0.62 us: shards(): jnp.concatenate([jnp.pad(padded_rows(rows, 1.0), ((0, 6), (0, 0))), jnp.p...]
where the time goes in v3:
time: 48.1 us; the launch traced here: 47.9 us
  Pallas kernels  47.3 us (98%)
  between operations  0.64 us (1%)
    pallas_call x1, Pallas kernels, shards(): pl.pallas_call(columns_kernel, out_shape=(jax.ShapeDtypeStruct((128, 8, 3...  44.5 us
    pallas_call x1, Pallas kernels, shards(): pl.pallas_call(slabs_kernel, grid=(8 // LATS,), out_shape=(jax.ShapeDtype...  2.84 us

profile of v3, /device:TPU:1, one launch (start us, length us, event | category | flops | bytes accessed | tf_op | source)
XLA Modules:
  0.0 47.9 jit_solution(11192369375504833011)
XLA Ops:
  0.6 44.5 %columns.1 = (f32[128,8,384]{2,1,0:T(8,128)}, f32[1536,128]{1,0:T(8,128)}) custom-call(s32[64]{0:T(128)} %band_index_ref.1, f32[8,254]{1,0:T(8,128)} %bitcast.8, f32[1,254]{1,0:T(1,128)} %bitcast.9, f32[9,2,127]{2,1,0:T(2,128)} %bitcast.7, s32[1,254]{1,0:T(1,128)} %bitcast.10, f32[8,96,254]{2,1,0:T(8,128)} %bitcast.6), custom_call_target="tpu_custom_call" | custom-call | tf_op jit(solution)/shard_map/columns/pallas_call | solution.py:740
  45.1 2.8 %slabs.1 = (f32[4,64,1536]{2,1,0:T(8,128)}, f32[8,96,254]{2,1,0:T(8,128)}) custom-call(f32[128,8,384]{2,1,0:T(8,128)} %get-tuple-element.6.arrived_ref, f32[1536,128]{1,0:T(8,128)} %get-tuple-element.7.low_ref.high_ref, f32[1536,128]{1,0:T(8,128)} %get-tuple-element.7.low_ref.high_ref), custom_call_target="tpu_custom_call" | custom-call | tf_op jit(solution)/shard_map/slabs/pallas_call | solution.py:818
